TPU v7x, 32 devices: a whole 2x2x4 slice. The times are simulated.
32 devices in a mesh: dp: 8 (over z, x), outer: 4 (over y, core).
Axes of the slice: x: 2, y: 2, z: 4, core: 2. Of those that a mesh axis runs over, the one named last changes fastest.
Arguments:
- partials: bfloat16 [4, 8, 2, 16, 8192], P('outer', 'dp'), may hold values from -3500 to 3500, as said below
- master: float32 [2, 16, 8192], P(None, 'dp'), may hold values from -6 to 6
- m_codes: bfloat16 [2, 16, 8192], P(None, 'dp'), may hold values from -1 to 1
- v_codes: bfloat16 [2, 16, 8192], P(None, 'dp'), may hold values from 0.049804688 to 1
- m_scales: float32 [2, 16, 4], P(None, 'dp'), may hold values from 0.0001 to 0.001
- v_scales: float32 [2, 16, 4], P(None, 'dp'), may hold values from 1e-08 to 1e-07
Outputs:
- new_master: float32 [2, 16, 8192], P(None, 'dp')
- new_m_codes: bfloat16 [2, 16, 8192], P(None, 'dp')
- new_v_codes: bfloat16 [2, 16, 8192], P(None, 'dp')
- new_m_scales: float32 [2, 16, 4], P(None, 'dp')
- new_v_scales: float32 [2, 16, 4], P(None, 'dp')
- weights: bfloat16 [2, 16, 8192], replicated
Inputs may be any that keep to these rules, and one draw needn't show every extreme that they name: Gradient partials of real values; entries vary from row to row and column to column.
All inputs are finite; a program needn't handle non-finite values. Where the computation divides by a largest or mean magnitude, that divisor is 1e-20 or more.
Results may differ from a plain program's by a relative error of at most 0.0004.
Values may be sent and summed in bfloat16 or wider, within the bound.
No kernel may reach another device: no remote copies, remote signals or barrier semaphores. Data moves between devices by JAX's collectives and lax.ppermute only.
A program may use at most 64 MiB of HBM per device.

v0:
```python
import jax
import jax.numpy as jnp
from jax import lax
from jax.sharding import PartitionSpec as P

BLOCK = 2048
STEP = 10


def adam_blocks(gradient, master, m_codes, v_codes, m_scales, v_scales, clip_factor):
    count = gradient.shape[0]
    rows = gradient.shape[1]
    blocks = gradient.shape[2] // BLOCK
    shape_four = (count, rows, blocks, BLOCK)
    moment = m_codes.astype(jnp.float32).reshape(shape_four) * m_scales[..., None]
    second = v_codes.astype(jnp.float32).reshape(shape_four) * v_scales[..., None]
    scaled = clip_factor * gradient.reshape(shape_four)
    moment = 0.9 * moment + 0.1 * scaled
    second = 0.95 * second + 0.05 * scaled * scaled
    update = moment / (1.0 - 0.9**STEP) / (jnp.sqrt(second / (1.0 - 0.95**STEP)) + 1e-08)
    fresh = master - 0.01 * update.reshape(master.shape)
    m_top = jnp.max(jnp.abs(moment), axis=3) + 1e-20
    v_top = jnp.max(jnp.abs(second), axis=3) + 1e-20
    m_next = (moment / m_top[..., None]).astype(jnp.bfloat16).reshape(master.shape)
    v_next = (second / v_top[..., None]).astype(jnp.bfloat16).reshape(master.shape)
    return (fresh, m_next, v_next, m_top, v_top, fresh.astype(jnp.bfloat16))


def body(partials, master, m_codes, v_codes, m_scales, v_scales):
    own_terms = partials[0, 0]
    row_part = lax.psum_scatter(
        own_terms.astype(jnp.float32), "dp", scatter_dimension=1, tiled=True
    )
    gradient = lax.psum(row_part, "outer")
    total = lax.psum(jnp.sum(gradient * gradient), "dp")
    clip_factor = 1.0 / jnp.maximum(jnp.sqrt(total), 1.0)
    results = adam_blocks(gradient, master, m_codes, v_codes, m_scales, v_scales, clip_factor)
    fresh, m_next, v_next, m_top, v_top, rounded = results
    weights = lax.all_gather(rounded, "dp", axis=1, tiled=True)
    return (fresh, m_next, v_next, m_top, v_top, weights)


def solution(mesh):
    return jax.shard_map(
        body,
        mesh=mesh,
        in_specs=(
            P("outer", "dp", None, None, None),
            P(None, "dp", None),
            P(None, "dp", None),
            P(None, "dp", None),
            P(None, "dp", None),
            P(None, "dp", None),
        ),
        out_specs=(
            P(None, "dp", None),
            P(None, "dp", None),
            P(None, "dp", None),
            P(None, "dp", None),
            P(None, "dp", None),
            P(),
        ),
        check_vma=False,
    )
```

profile of v0, /device:TPU:0, one launch (start us, length us, event | category | flops | bytes accessed | tf_op | source)
XLA Modules:
  0.0 194.2 jit_solution(15518864114638072132)
XLA Ops:
  7.2 2.1 %bitcast_convert_fusion = f32[2,16,8192]{2,1,0:T(8,128)} fusion(bf16[1,1,2,16,8192]{4,3,2,1,0:T(8,128)(2,1)} %param.6), kind=kLoop, calls=%fused_computation | loop fusion | flops 262144 | bytes 1572864 | tf_op jit(solution)/shard_map/convert_element_type | solution.py:32
  9.4 0.6 copy-done.8
  10.1 0.6 dynamic-slice
  11.3 81.3 %all-reduce.6.cloned.1.call-done = f32[2,16,8192]{2,1,0:T(8,128)} async-done(((f32[2,16,8192]{2,1,0:T(8,128)}), f32[2,16,8192]{2,1,0:T(8,128)}) %all-reduce.6.cloned.1.call-update) | async-done | bytes 1048592
  92.6 1.7 constant_dynamic-slice_fusion
  94.4 0.7 copy-done.5
  95.1 0.1 mul.105
  95.3 0.5 copy-done.4
  95.9 0.1 mul.115
  96.0 0.7 copy-done.1
  96.8 30.1 %all-reduce.4.cloned.1.call-done = f32[2,2,8192]{2,1,0:T(2,128)} async-done(((f32[2,2,8192]{2,1,0:T(2,128)}), f32[2,2,8192]{2,1,0:T(2,128)}) %all-reduce.4.cloned.1.call-update) | async-done | bytes 131088 | tf_op jit(solution)/shard_map/psum | solution.py:34
  126.9 1.7 multiply_reduce_fusion
  128.6 22.0 %psum.15 = f32[]{:T(128)} all-reduce(f32[]{:T(128)} %multiply_reduce_fusion), channel_id=1, replica_groups=mesh['dp'=8,'outer'=4] {'dp'}, use_global_device_ids=true, to_apply=%region_3.0 | all-reduce | flops 1 | bytes 8 | tf_op jit(solution)/shard_map/psum | solution.py:35
  151.4 1.1 fusion.4
  152.5 0.1 mul.127
  152.6 0.3 fusion.3
  152.9 0.1 div.47
  153.0 0.5 copy-done.7
  153.5 0.1 div.48
  153.6 0.1 div.50
  153.7 0.1 div.51
  153.9 31.4 %all_gather.3 = bf16[2,16,8192]{2,0,1:T(2,128)(2,1)S(1)} all-gather(bf16[2,2,8192]{2,0,1:T(2,128)(2,1)S(1)} %copy.12), channel_id=1, replica_groups=mesh['dp'=8,'outer'=4] {'dp'}, dimensions={1}, use_global_device_ids=true | all-gather | bytes 589824 | tf_op jit(solution)/shard_map/all_gather | solution.py:39
  185.3 1.1 copy.13
  186.4 1.0 divide_convert_fusion
  (23 shorter events, 0.5 us)
Async XLA Ops:
  7.2 85.4 %all-reduce.6.cloned.1.call-start = ((), (), s32[]{:S(2)}) async-start(), calls=%async_computation.1 | async-start | bytes 2097152
  9.4 117.5 %all-reduce.4.cloned.1.call-start = ((), (), s32[]{:S(2)}) async-start(), calls=%async_computation | async-start | bytes 262144 | tf_op jit(solution)/shard_map/psum | solution.py:34
  9.4 0.7 copy-start.8
  94.3 0.7 copy-start.5
  95.1 0.7 copy-start.4
  95.9 0.8 copy-start.1
  96.8 31.8 %copy-start = (bf16[2,2,8192]{2,1,0:T(2,128)(2,1)S(1)}, bf16[2,2,8192]{2,1,0:T(2,128)(2,1)}, u32[]{:S(2)}) copy-start(bf16[2,2,8192]{2,1,0:T(2,128)(2,1)} %param.9) | copy-start | bytes 196612
  126.9 24.5 %copy-start.3 = (f32[2,2,8192]{2,1,0:T(2,128)S(1)}, f32[2,2,8192]{2,1,0:T(2,128)}, u32[]{:S(2)}) copy-start(f32[2,2,8192]{2,1,0:T(2,128)} %param.7) | copy-start | bytes 393220
  128.6 22.8 %copy-start.2 = (f32[2,2,8192]{2,1,0:T(2,128)S(1)}, f32[2,2,8192]{2,1,0:T(2,128)}, u32[]{:S(2)}) copy-start(f32[2,2,8192]{2,1,0:T(2,128)} %all-reduce.4.cloned.1.call-done) | copy-start | bytes 393220
  152.9 0.6 copy-start.7
  152.9 0.7 copy-start.6
Sparse Core Ops, SparseCore 0:
  11.5 81.0 all-reduce.5
  95.5 31.3 all-reduce.3
where the time goes:
time: 195 us; the launch traced here: 194 us
  waiting for transfers between devices  111 us (57%)
  blocking collectives  53.4 us (27%)
  between operations  15.6 us (8%)
  local copies, waits for them, and re-layouts  7.63 us (4%)
  other arithmetic  6.17 us (3%)
    unnamed x3, waiting for transfers between devices  81.3 us
    all_gather x1, blocking collectives, body(): weights = lax.all_gather(rounded, 'dp', axis=1, tiled=True)  31.4 us
    psum x1, waiting for transfers between devices, body(): gradient = lax.psum(row_part, 'outer')  30.1 us
    psum x1, blocking collectives, body(): total = lax.psum(jnp.sum(gradient * gradient), 'dp')  22 us
    unnamed x21, local copies, waits for them, and re-layouts  6.46 us
  transfers between devices with their start and end apart: 2, of which 2 were waited for; matrix products, arithmetic and copies ran while one was open for 1% of the time, Pallas kernels for 0%

commit v1 on v0

v1 whole, which is shorter than its diff:
```python
import jax
import jax.numpy as jnp
from jax import lax
from jax.sharding import PartitionSpec as P

BLOCK = 2048
STEP = 10


def adam_blocks(gradient, master, m_codes, v_codes, m_scales, v_scales, clip_factor):
    count, rows, width = gradient.shape
    shape_four = (count, rows, width // BLOCK, BLOCK)
    moment = m_codes.astype(jnp.float32).reshape(shape_four) * m_scales[..., None]
    second = v_codes.astype(jnp.float32).reshape(shape_four) * v_scales[..., None]
    scaled = clip_factor * gradient.reshape(shape_four)
    moment = 0.9 * moment + 0.1 * scaled
    second = 0.95 * second + 0.05 * scaled * scaled
    update = moment / (1.0 - 0.9**STEP) / (jnp.sqrt(second / (1.0 - 0.95**STEP)) + 1e-08)
    fresh = master - 0.01 * update.reshape(master.shape)
    m_top = jnp.max(jnp.abs(moment), axis=3) + 1e-20
    v_top = jnp.max(jnp.abs(second), axis=3) + 1e-20
    m_next = (moment / m_top[..., None]).astype(jnp.bfloat16).reshape(master.shape)
    v_next = (second / v_top[..., None]).astype(jnp.bfloat16).reshape(master.shape)
    return (fresh, m_next, v_next, m_top, v_top, fresh.astype(jnp.bfloat16))


def flip(value, axis, size, bit):
    return lax.ppermute(value, axis, [(i, i ^ bit) for i in range(size)])


def make_body(dp_n, outer_n):
    both = ("dp", "outer")

    def body(partials, master, m_codes, v_codes, m_scales, v_scales):
        own = partials[0, 0]
        count, rows_all, width = own.shape
        rows = rows_all // dp_n
        part = width // outer_n
        outer_at = lax.axis_index("outer")
        pieces = own.reshape(count, dp_n, rows, outer_n, part)
        pieces = pieces.transpose(1, 3, 0, 2, 4).reshape(dp_n * outer_n, count * rows, part)
        got = lax.all_to_all(pieces, both, 0, 0, tiled=True)
        piece = jnp.sum(got.astype(jnp.float32), axis=0)
        square = jnp.sum(piece * piece)
        held = piece[None]
        bit = 1
        while bit < outer_n:
            other = flip(held, "outer", outer_n, bit)
            held = jnp.concatenate([held, other], axis=0)
            bit *= 2
        squares = lax.all_to_all(
            jnp.broadcast_to(square, (dp_n * outer_n, 8, 128)), both, 0, 0, tiled=True
        )
        total = jnp.sum(squares[:, 0, 0])
        clip_factor = 1.0 / jnp.maximum(jnp.sqrt(total), 1.0)
        order = [lax.dynamic_index_in_dim(held, j ^ outer_at, 0, keepdims=False) for j in range(outer_n)]
        gradient = jnp.stack(order, axis=1).reshape(count, rows, width)
        results = adam_blocks(gradient, master, m_codes, v_codes, m_scales, v_scales, clip_factor)
        fresh, m_next, v_next, m_top, v_top, rounded = results
        side = outer_at % 2
        mine = lax.dynamic_index_in_dim(rounded, side, 0, keepdims=False)
        mine = lax.all_to_all(
            jnp.broadcast_to(mine, (dp_n, rows, width)), "dp", 0, 0, tiled=True
        ).reshape(rows_all, width)
        other = flip(mine, "outer", outer_n, 1)
        weights = jnp.where(side == 0, jnp.stack([mine, other]), jnp.stack([other, mine]))
        return (fresh, m_next, v_next, m_top, v_top, weights)

    return body


def solution(mesh):
    rows = P(None, "dp", None)
    return jax.shard_map(
        make_body(mesh.shape["dp"], mesh.shape["outer"]),
        mesh=mesh,
        in_specs=(P("outer", "dp", None, None, None), rows, rows, rows, rows, rows),
        out_specs=(rows, rows, rows, rows, rows, P()),
        check_vma=False,
    )
```

time: 195 us -> 63.4 us (0.33)
  waiting for transfers between devices: 111 us -> 9.37 us
  blocking collectives: 53.4 us -> 34.7 us
  between operations: 15.6 us -> 1.64 us
  starting transfers between devices: 0.08 us -> 3.75 us
  other arithmetic: 6.17 us -> 4.02 us
    unnamed x3 -> x0, waiting for transfers between devices: 81.3 us -> none
    all_to_all x0 -> x2, blocking collectives: none -> 34.7 us  [the longest x1 22.7 us: body(): got = lax.all_to_all(pieces, both, 0, 0, tiled=True)]
    all_gather x1 -> x0, blocking collectives: 31.4 us -> none  [body(): weights = lax.all_gather(rounded, 'dp', axis=1, tiled=True)]
    psum x1 -> x0, waiting for transfers between devices: 30.1 us -> none  [body(): gradient = lax.psum(row_part, 'outer')]
    psum x1 -> x0, blocking collectives: 22 us -> none  [body(): total = lax.psum(jnp.sum(gradient * gradient), 'dp')]
    all_to_all x0 -> x1, waiting for transfers between devices: none -> 7.96 us  [body(): lax.all_to_all(jnp.broadcast_to(square, (dp_n * outer_n, 8, 128)), both,...]
    convert_element_type x2 -> x0, other arithmetic: 3.26 us -> none  [the longest x1 2.14 us: body(): own_terms.astype(jnp.float32)]
    all_to_all x0 -> x1, starting transfers between devices: none -> 2.7 us  [body(): lax.all_to_all(jnp.broadcast_to(square, (dp_n * outer_n, 8, 128)), both,...]
  transfers between devices with their start and end apart: 2 -> 4, of which waited for: 2 -> 2; matrix products, arithmetic and copies ran while one was open for 1% -> 4% of each run, Pallas kernels for 0% -> 0%
where the time goes in v1:
time: 63.4 us; the launch traced here: 63 us
  blocking collectives  34.7 us (55%)
  local copies, waits for them, and re-layouts  9.49 us (15%)
  waiting for transfers between devices  9.37 us (15%)
  other arithmetic  4.02 us (6%)
  starting transfers between devices  3.75 us (6%)
  between operations  1.64 us (3%)
    all_to_all x1, blocking collectives, body(): got = lax.all_to_all(pieces, both, 0, 0, tiled=True)  22.7 us
    all_to_all x1, blocking collectives, body(): lax.all_to_all(jnp.broadcast_to(mine, (dp_n, rows, width)), 'dp', 0, 0, t...  12 us
    all_to_all x1, waiting for transfers between devices, body(): lax.all_to_all(jnp.broadcast_to(square, (dp_n * outer_n, 8, 128)), both,...  7.96 us
    unnamed x16, local copies, waits for them, and re-layouts  4.37 us
    all_to_all x1, starting transfers between devices, body(): lax.all_to_all(jnp.broadcast_to(square, (dp_n * outer_n, 8, 128)), both,...  2.7 us
    another operation x2, local copies, waits for them, and re-layouts, body(): pieces = own.reshape(count, dp_n, rows, outer_n, part)  1.68 us
    ppermute x3, waiting for transfers between devices, flip(): return lax.ppermute(value, axis, [(i, i ^ bit) for i in range(size)])  1.41 us
    broadcast_in_dim x1, local copies, waits for them, and re-layouts, body(): jnp.broadcast_to(square, (dp_n * outer_n, 8, 128))  1.31 us
  transfers between devices with their start and end apart: 4, of which 2 were waited for; matrix products, arithmetic and copies ran while one was open for 4% of the time, Pallas kernels for 0%

profile of v1, /device:TPU:0, one launch (start us, length us, event | category | flops | bytes accessed | tf_op | source)
XLA Modules:
  0.0 63.0 jit_solution(3174491038910075539)
XLA Ops:
  0.6 1.4 %reshape_squeeze.3 = bf16[2,8,2,4,2048]{4,3,2,1,0:T(4,128)(2,1)S(1)} reshape(bf16[1,1,2,16,8192]{4,3,2,1,0:T(8,128)(2,1)} %param.6) | data formatting | bytes 1048576 | tf_op jit(solution)/shard_map/reshape;squeeze | solution.py:40
  2.1 0.2 copy.22
  2.4 0.4 copy.18
  2.9 22.7 %all_to_all.15 = bf16[32,4,2048]{2,1,0:T(4,128)(2,1)S(1)} all-to-all(bf16[32,4,2048]{2,1,0:T(4,128)(2,1)S(1)} %copy.18), channel_id=1, replica_groups=mesh['dp'=8,'outer'=4] {'dp','outer'}, dimensions={0} | all-to-all | bytes 1048576 | tf_op jit(solution)/shard_map/all_to_all | solution.py:42
  25.6 0.2 convert_reduce_fusion
  26.0 0.7 %copy-done.1 = bf16[2,2,8192]{2,1,0:T(2,128)(2,1)S(1)} copy-done((bf16[2,2,8192]{2,1,0:T(2,128)(2,1)S(1)}, bf16[2,2,8192]{2,1,0:T(2,128)(2,1)}, u32[]{:S(2)}) %copy-start.1) | copy-done | bytes 65560
  26.7 0.8 %copy-done = bf16[2,2,8192]{2,1,0:T(2,128)(2,1)S(1)} copy-done((bf16[2,2,8192]{2,1,0:T(2,128)(2,1)S(1)}, bf16[2,2,8192]{2,1,0:T(2,128)(2,1)}, u32[]{:S(2)}) %copy-start) | copy-done | bytes 65560
  27.6 0.6 copy-done.5
  28.4 0.5 copy-done.4
  29.3 0.9 %collective-permute-start.1 = (f32[2,4,2048]{2,0,1:T(2,128)S(1)}, f32[2,4,2048]{2,0,1:T(2,128)S(1)}, u32[]{:S(2)}, u32[]{:S(2)}) collective-permute-start(f32[2,4,2048]{2,0,1:T(2,128)S(1)} %pad_maximum_fusion.1), channel_id=1, source_target_pairs={{0,2},{1,3},{2,0},{3,1},{4,6},{5,7},{6,4},{7,5},{8,10},{9,11},{10,... | collective-permute-start | bytes 196616 | tf_op jit(solution)/shard_map/ppermute | solution.py:28
  30.2 0.6 multiply_reduce_fusion
  30.8 1.3 %broadcast_in_dim.6 = f32[32,8,128]{2,1,0:T(8,128)} broadcast(f32[]{:T(128)} %multiply_reduce_fusion), dimensions={} | broadcast | bytes 131076 | tf_op jit(solution)/shard_map/broadcast_in_dim | solution.py:52
  32.1 2.7 %all-to-all-start.1 = ((f32[32,8,128]{2,1,0:T(8,128)}), f32[32,8,128]{2,1,0:T(8,128)S(1)}, u32[]{:S(2)}, u32[]{:S(2)}) async-start(f32[32,8,128]{2,1,0:T(8,128)} %broadcast_in_dim.6), calls=%async_computation.1 | async-start | bytes 262144 | tf_op jit(solution)/shard_map/all_to_all | solution.py:51
  35.1 8.0 %all-to-all-done.1 = f32[32,8,128]{2,1,0:T(8,128)S(1)} async-done(((f32[32,8,128]{2,1,0:T(8,128)}), f32[32,8,128]{2,1,0:T(8,128)S(1)}, u32[]{:S(2)}, u32[]{:S(2)}) %all-to-all-start.1) | async-done | bytes 131104 | tf_op jit(solution)/shard_map/all_to_all | solution.py:51
  43.0 0.6 %slice_reduce_fusion = f32[]{:T(128)} fusion(f32[32,8,128]{2,1,0:T(8,128)S(1)} %all-to-all-done.1), kind=kLoop, calls=%fused_computation.21 | loop fusion | flops 31 | bytes 132 | tf_op jit(solution)/shard_map/reduce_sum | solution.py:54
  44.4 0.3 fusion.3
  44.8 0.5 copy-done.7
  45.8 0.8 %copy-done.3 = f32[2,2,8192]{2,1,0:T(2,128)S(1)} copy-done((f32[2,2,8192]{2,1,0:T(2,128)S(1)}, f32[2,2,8192]{2,1,0:T(2,128)}, u32[]{:S(2)}) %copy-start.3) | copy-done | bytes 131096
  46.6 1.2 %divide_convert_fusion = (bf16[2,2,8192]{2,1,0:T(2,128)(2,1)}, f32[2,2,8192]{2,1,0:T(2,128)S(1)}, bf16[2,2,8192]{2,1,0:T(2,128)(2,1)}) fusion(f32[2,2,8192]{2,1,0:T(2,128)S(1)} %div.51, f32[2,2,8192]{2,1,0:T(2,128)S(1)} %mul.112, f32[2,2,8192]{2,1,0:T(2,128)S(1)} %mul.116, bf16[2,2,8192]{2,1,0:T(2,128)(2,1)S(1)} %copy-done, f32[2,2,8192]{2,1,0:T(2,128)S(1)} %copy-done.3, ...), kind=kLoop, calls=%fused_computation.15 | loop fusion | flops 688128 | bytes 1179648 | tf_op jit(solution)/shard_map/convert_element_type | solution.py:23
  47.8 0.1 broadcast_in_dim.15
  48.0 0.5 copy-done.2
  48.4 12.0 %all_to_all.16 = bf16[8,2,8192]{2,1,0:T(2,128)(2,1)S(1)} all-to-all(bf16[8,2,8192]{2,1,0:T(2,128)(2,1)S(1)} %broadcast_in_dim.15), channel_id=1, replica_groups=mesh['dp'=8,'outer'=4] {'dp'}, dimensions={0} | all-to-all | bytes 524288 | tf_op jit(solution)/shard_map/all_to_all | solution.py:62
  60.7 1.4 %collective-permute-done.2 = bf16[16,8192]{1,0:T(8,128)(2,1)S(1)} collective-permute-done((bf16[16,8192]{1,0:T(8,128)(2,1)S(1)}, bf16[16,8192]{1,0:T(8,128)(2,1)S(1)}, u32[]{:S(2)}, u32[]{:S(2)}) %collective-permute-start.2) | collective-permute-done | bytes 262176 | tf_op jit(solution)/shard_map/ppermute | solution.py:28
  62.1 0.9 %maximum_select_fusion = bf16[2,16,8192]{2,1,0:T(8,128)(2,1)} fusion(bf16[1,16,8192]{2,1,0:T(8,128)(2,1)S(1)} %bitcast.15, bf16[1,16,8192]{2,1,0:T(8,128)(2,1)S(1)} %stack_reshape.4, pred[]{:T(512)S(6)} %eq.5), kind=kLoop, calls=%fused_computation.1 | loop fusion | flops 786432 | bytes 1048577 | tf_op jit(solution)/shard_map/jit(_where)/select_n | solution.py:66
  (33 shorter events, 1.9 us)
Async XLA Ops:
  25.8 0.8 %copy-start.1 = (bf16[2,2,8192]{2,1,0:T(2,128)(2,1)S(1)}, bf16[2,2,8192]{2,1,0:T(2,128)(2,1)}, u32[]{:S(2)}) copy-start(bf16[2,2,8192]{2,1,0:T(2,128)(2,1)} %param.8) | copy-start | bytes 196612
  25.9 3.3 %collective-permute-start = (f32[1,4,2048]{2,0,1:T(1,128)S(1)}, f32[1,4,2048]{2,0,1:T(1,128)S(1)}, u32[]{:S(2)}, u32[]{:S(2)}) collective-permute-start(f32[1,4,2048]{2,0,1:T(1,128)S(1)} %broadcast_in_dim.14), channel_id=1, source_target_pairs={{0,1},{1,0},{2,3},{3,2},{4,5},{5,4},{6,7},{7,6},{8,9},{9,8},{10,11... | collective-permute-start | bytes 98312 | tf_op jit(solution)/shard_map/ppermute | solution.py:28
  26.7 0.8 %copy-start = (bf16[2,2,8192]{2,1,0:T(2,128)(2,1)S(1)}, bf16[2,2,8192]{2,1,0:T(2,128)(2,1)}, u32[]{:S(2)}) copy-start(bf16[2,2,8192]{2,1,0:T(2,128)(2,1)} %param.9) | copy-start | bytes 196612
  27.5 0.7 %copy-start.5 = (f32[2,2,4]{2,1,0:T(2,128)S(1)}, f32[2,2,4]{2,1,0:T(2,128)}, u32[]{:S(2)}) copy-start(f32[2,2,4]{2,1,0:T(2,128)} %param.10) | copy-start | bytes 196
  28.3 0.7 %copy-start.4 = (f32[2,2,4]{2,1,0:T(2,128)S(1)}, f32[2,2,4]{2,1,0:T(2,128)}, u32[]{:S(2)}) copy-start(f32[2,2,4]{2,1,0:T(2,128)} %param.11) | copy-start | bytes 196
  29.3 5.5 %collective-permute-start.1 = (f32[2,4,2048]{2,0,1:T(2,128)S(1)}, f32[2,4,2048]{2,0,1:T(2,128)S(1)}, u32[]{:S(2)}, u32[]{:S(2)}) collective-permute-start(f32[2,4,2048]{2,0,1:T(2,128)S(1)} %pad_maximum_fusion.1), channel_id=1, source_target_pairs={{0,2},{1,3},{2,0},{3,1},{4,6},{5,7},{6,4},{7,5},{8,10},{9,11},{10,... | collective-permute-start | bytes 196616 | tf_op jit(solution)/shard_map/ppermute | solution.py:28
  32.1 10.9 %all-to-all-start.1 = ((f32[32,8,128]{2,1,0:T(8,128)}), f32[32,8,128]{2,1,0:T(8,128)S(1)}, u32[]{:S(2)}, u32[]{:S(2)}) async-start(f32[32,8,128]{2,1,0:T(8,128)} %broadcast_in_dim.6), calls=%async_computation.1 | async-start | bytes 262144 | tf_op jit(solution)/shard_map/all_to_all | solution.py:51
  44.8 0.6 copy-start.7
  44.8 0.7 %copy-start.6 = (f32[2,2,4]{2,1,0:T(2,128)}, f32[2,2,4]{2,1,0:T(2,128)S(1)}, u32[]{:S(2)}) copy-start(f32[2,2,4]{2,1,0:T(2,128)S(1)} %get-tuple-element.16) | copy-start | bytes 196
  45.7 0.9 %copy-start.3 = (f32[2,2,8192]{2,1,0:T(2,128)S(1)}, f32[2,2,8192]{2,1,0:T(2,128)}, u32[]{:S(2)}) copy-start(f32[2,2,8192]{2,1,0:T(2,128)} %param.7) | copy-start | bytes 393220
  47.8 0.7 %copy-start.2 = (f32[2,2,8192]{2,1,0:T(2,128)}, f32[2,2,8192]{2,1,0:T(2,128)S(1)}, u32[]{:S(2)}) copy-start(f32[2,2,8192]{2,1,0:T(2,128)S(1)} %get-tuple-element.10) | copy-start | bytes 393220
  60.5 1.6 %collective-permute-start.2 = (bf16[16,8192]{1,0:T(8,128)(2,1)S(1)}, bf16[16,8192]{1,0:T(8,128)(2,1)S(1)}, u32[]{:S(2)}, u32[]{:S(2)}) collective-permute-start(bf16[16,8192]{1,0:T(8,128)(2,1)S(1)} %reshape.61), channel_id=1, source_target_pairs={{0,1},{1,0},{2,3},{3,2},{4,5},{5,4},{6,7},{7,6},{8,9},{9,8},{10,11... | collective-permute-start | bytes 786440 | tf_op jit(solution)/shard_map/ppermute | solution.py:28

commit v2 on v1

v2 whole, which is shorter than its diff:
```python
import jax
import jax.numpy as jnp
from jax import lax
from jax.experimental import pallas as pl
from jax.experimental.pallas import tpu as pltpu
from jax.sharding import PartitionSpec as P

BLOCK = 2048
STEP = 10
LANES = 128
SUBLANES = 8
NEAR_BYTES = 768 * 1024
BOTH = ("dp", "outer")
FIRST_FIX = 1.0 / (1.0 - 0.9**STEP)
SECOND_FIX = 1.0 / (1.0 - 0.95**STEP)


def sum_kernel(got_ref, piece_ref, square_ref):
    terms = got_ref.shape[0]
    group = 8

    def some(i):
        return jnp.sum(got_ref[pl.ds(i * group, group)].astype(jnp.float32), axis=0)

    total = some(0)
    if terms <= 4 * group:
        for i in range(1, terms // group):
            total = total + some(i)
    else:
        total = lax.fori_loop(1, terms // group, lambda i, held: held + some(i), total)
    piece_ref[...] = total
    lanes = jnp.sum(total * total, axis=0, keepdims=True)
    square_ref[...] = jnp.broadcast_to(lanes[None], square_ref.shape)


def prep_kernel(m_ref, v_ref, ms_ref, vs_ref, m_out_ref, v_out_ref):
    count, rows, blocks = ms_ref.shape
    span = BLOCK // LANES * rows
    for at in range(count):
        for block in range(blocks):
            here = pl.ds(block * span, span)
            for code_ref, scale_ref, decay, out_ref in (
                (m_ref, ms_ref, 0.9, m_out_ref),
                (v_ref, vs_ref, 0.95, v_out_ref),
            ):
                scale = scale_ref[at, :, block : block + 1]
                scale = jnp.concatenate([scale] * (span // rows), axis=0)
                out_ref[at, here, :] = decay * (code_ref[at, here, :].astype(jnp.float32) * scale)


def clip_of(square_ref):
    total = jnp.sum(jnp.sum(square_ref[...], axis=0), axis=1, keepdims=True)
    return 1.0 / jnp.maximum(jnp.sqrt(total), 1.0)


def moments(clip, piece_ref, m_ref, v_ref, at, start, here, span):
    g = clip * piece_ref[pl.ds(start, span), :]
    return m_ref[at, here, :] + 0.1 * g, v_ref[at, here, :] + 0.05 * g * g


def fresh_of(master_ref, at, here, m, v):
    update = (m * FIRST_FIX) / (jnp.sqrt(v * SECOND_FIX) + 1e-08)
    return master_ref[at, here, :] - 0.01 * update


def weight_kernel(square_ref, master_ref, m_ref, v_ref, *refs):
    *piece_refs, out_ref = refs
    outer_at = lax.axis_index("outer")
    side = outer_at % 2
    held = piece_refs[0].shape[0] // master_ref.shape[0]
    clip = clip_of(square_ref)
    for offset, piece_ref in enumerate(piece_refs):
        here = pl.ds(pl.multiple_of((outer_at ^ offset) * held, SUBLANES), held)
        start = pl.multiple_of(side * held, SUBLANES)
        m, v = moments(clip, piece_ref, m_ref, v_ref, side, start, here, held)
        fresh = fresh_of(master_ref, side, here, m, v).astype(jnp.bfloat16)
        out_ref[:, here, :] = jnp.broadcast_to(fresh[None], (out_ref.shape[0],) + fresh.shape)


def state_kernel(rows, square_ref, master_ref, m_ref, v_ref, *refs):
    *piece_refs, fresh_ref, m_next_ref, v_next_ref, m_top_ref, v_top_ref = refs
    outer_at = lax.axis_index("outer")
    count = master_ref.shape[0]
    span = BLOCK // LANES * rows
    held = piece_refs[0].shape[0] // count
    clip = clip_of(square_ref)
    columns = lax.broadcasted_iota(jnp.int32, m_top_ref.shape[1:], 1)

    def top_of(value):
        top = jnp.max(jnp.abs(value).reshape(span // SUBLANES, SUBLANES, LANES), axis=0)
        step = rows
        while step < SUBLANES:
            top = jnp.maximum(top, pltpu.roll(top, step, 0))
            step *= 2
        return jnp.max(top, axis=1, keepdims=True) + 1e-20

    def scaled(value, top):
        tiles = value.reshape(span // SUBLANES, SUBLANES, LANES)
        return (tiles * (1.0 / top)).reshape(span, LANES).astype(jnp.bfloat16)

    for at in range(count):
        m_tops = v_tops = jnp.zeros(m_top_ref.shape[1:], jnp.float32)
        for offset, piece_ref in enumerate(piece_refs):
            for inner in range(held // span):
                block = (outer_at ^ offset) * (held // span) + inner
                here = pl.ds(pl.multiple_of(block * span, SUBLANES), span)
                m, v = moments(clip, piece_ref, m_ref, v_ref, at, at * held + inner * span, here, span)
                fresh_ref[at, here, :] = fresh_of(master_ref, at, here, m, v)
                m_top, v_top = top_of(m), top_of(v)
                m_next_ref[at, here, :] = scaled(m, m_top)
                v_next_ref[at, here, :] = scaled(v, v_top)
                m_tops = jnp.where(columns == block, m_top[:rows], m_tops)
                v_tops = jnp.where(columns == block, v_top[:rows], v_tops)
        m_top_ref[at] = m_tops
        v_top_ref[at] = v_tops


def near(value):
    if value.size * value.dtype.itemsize > NEAR_BYTES:
        return value
    return pltpu.with_memory_space_constraint(value, pltpu.VMEM)


def call(kernel, outs, args, near_in=True, near_out=True):
    def shape_of(shape, dtype):
        plain_shape = jax.ShapeDtypeStruct(shape, dtype)
        small = plain_shape.size * plain_shape.dtype.itemsize <= NEAR_BYTES
        return pltpu.VMEM(shape, dtype) if near_out and small else plain_shape

    spec = pl.BlockSpec(memory_space=pltpu.VMEM)
    return pl.pallas_call(
        kernel,
        out_shape=[shape_of(*out) for out in outs],
        in_specs=[spec] * len(args),
        out_specs=[spec] * len(outs),
    )(*[near(a) if near_in else a for a in args])


def dense(value):
    count, rows, width = value.shape
    tiles = value.reshape(count, rows, width // LANES, LANES).transpose(0, 2, 1, 3)
    return tiles.reshape(count, width // LANES * rows, LANES)


def plain(value, rows):
    count, tall, lanes = value.shape
    tiles = value.reshape(count, tall // rows, rows, lanes).transpose(0, 2, 1, 3)
    return tiles.reshape(count, rows, tall // rows * lanes)


def flip(value, size, bit):
    return lax.ppermute(value, "outer", [(i, i ^ bit) for i in range(size)])


def make_body(dp_n, outer_n):
    f32, bf16 = jnp.float32, jnp.bfloat16

    def body(partials, master, m_codes, v_codes, m_scales, v_scales):
        own = partials[0, 0]
        count, rows_all, width = own.shape
        rows = rows_all // dp_n
        total_n = dp_n * outer_n
        tiles = width // LANES
        part = tiles // outer_n
        tall = (count, tiles * rows, LANES)
        pieces = own.reshape(count, dp_n, rows, outer_n, part, LANES)
        pieces = pieces.transpose(1, 3, 0, 4, 2, 5).reshape(total_n, count * part * rows, LANES)
        got = lax.all_to_all(pieces, BOTH, 0, 0, tiled=True)
        m_part, v_part = call(
            prep_kernel, [(tall, f32), (tall, f32)],
            [dense(m_codes), dense(v_codes), m_scales, v_scales], near_in=False,
        )
        piece, square = call(sum_kernel, [(got.shape[1:], f32), ((total_n, 1, LANES), f32)], [got])
        squares = lax.all_to_all(square, BOTH, 0, 0, tiled=True)
        held = {0: piece}
        bit = outer_n // 2
        while bit:
            for at in list(held):
                held[at ^ bit] = flip(held[at], outer_n, bit)
            bit //= 2
        args = [squares, dense(master), m_part, v_part] + [held[i] for i in range(outer_n)]
        (mine,) = call(weight_kernel, [((dp_n, tiles * rows, LANES), bf16)], args)
        mine = lax.all_to_all(mine, "dp", 0, 0, tiled=True)
        fresh, m_next, v_next, m_top, v_top = call(
            lambda *refs: state_kernel(rows, *refs),
            [(tall, f32), (tall, bf16), (tall, bf16), (m_scales.shape, f32), (v_scales.shape, f32)],
            args, near_out=False,
        )
        mine = mine.reshape(dp_n, tiles, rows, LANES).transpose(0, 2, 1, 3).reshape(rows_all, width)
        other = flip(mine, outer_n, 1)
        side = lax.axis_index("outer") % 2
        weights = jnp.where(side == 0, jnp.stack([mine, other]), jnp.stack([other, mine]))
        return (plain(fresh, rows), plain(m_next, rows), plain(v_next, rows), m_top, v_top, weights)

    return body


def solution(mesh):
    rows = P(None, "dp", None)
    outer_n = mesh.shape["outer"]
    return jax.shard_map(
        make_body(mesh.shape["dp"], outer_n),
        mesh=mesh,
        in_specs=(P("outer", "dp", None, None, None), rows, rows, rows, rows, rows),
        out_specs=(rows, rows, rows, rows, rows, P()),
        check_vma=False,
    )
```

time: 63.4 us -> 54.7 us (0.86)
  local copies, waits for them, and re-layouts: 9.49 us -> 2.03 us
  other arithmetic: 4.02 us -> 0.87 us
  Pallas kernels: 0 us -> 2.82 us
  between operations: 1.64 us -> 0.72 us
    unnamed x16 -> x4, local copies, waits for them, and re-layouts: 4.37 us -> 1.33 us
    pallas_call x0 -> x4, Pallas kernels: none -> 2.82 us  [call(): pl.pallas_call(kernel, out_shape=[shape_of(*out) for out in outs], in_spe...]
    ppermute x3 -> x4, waiting for transfers between devices: 1.41 us -> 3.39 us  [flip(): return lax.ppermute(value, 'outer', [(i, i ^ bit) for i in range(size)])]
    all_to_all x1, waiting for transfers between devices: 7.96 us -> 6.12 us  [body(): squares = lax.all_to_all(square, BOTH, 0, 0, tiled=True)]
    reduce_sum x3 -> x0, other arithmetic: 1.47 us -> none  [the longest x1 0.63 us: body(): total = jnp.sum(squares[:, 0, 0])]
    broadcast_in_dim x3 -> x0, local copies, waits for them, and re-layouts: 1.47 us -> none  [the longest x1 1.31 us: body(): jnp.broadcast_to(square, (dp_n * outer_n, 8, 128))]
    convert_element_type x1 -> x0, other arithmetic: 1.17 us -> none  [adam_blocks(): (second / v_top[..., None]).astype(jnp.bfloat16).reshape(master.shape)]
    another operation x2 -> x1, local copies, waits for them, and re-layouts: 1.68 us -> 0.54 us  [body(): pieces = own.reshape(count, dp_n, rows, outer_n, part, LANES)]
  transfers between devices with their start and end apart: 4 -> 5, of which waited for: 2 -> 3; matrix products, arithmetic and copies ran while one was open for 4% -> 0% of each run, Pallas kernels for 0% -> 4%
where the time goes in v2:
time: 54.7 us; the launch traced here: 54.5 us
  blocking collectives  34.4 us (63%)
  waiting for transfers between devices  9.51 us (17%)
  starting transfers between devices  4.1 us (7%)
  Pallas kernels  2.82 us (5%)
  local copies, waits for them, and re-layouts  2.03 us (4%)
  other arithmetic  0.87 us (2%)
  between operations  0.72 us (1%)
    all_to_all x1, blocking collectives, body(): got = lax.all_to_all(pieces, BOTH, 0, 0, tiled=True)  22.7 us
    all_to_all x1, blocking collectives, body(): mine = lax.all_to_all(mine, 'dp', 0, 0, tiled=True)  11.6 us
    all_to_all x1, waiting for transfers between devices, body(): squares = lax.all_to_all(square, BOTH, 0, 0, tiled=True)  6.12 us
    ppermute x4, waiting for transfers between devices, flip(): return lax.ppermute(value, 'outer', [(i, i ^ bit) for i in range(size)])  3.39 us
    all_to_all x1, starting transfers between devices, body(): squares = lax.all_to_all(square, BOTH, 0, 0, tiled=True)  3.09 us
    pallas_call x4, Pallas kernels, call(): pl.pallas_call(kernel, out_shape=[shape_of(*out) for out in outs], in_spe...  2.82 us
    unnamed x4, local copies, waits for them, and re-layouts  1.33 us
  transfers between devices with their start and end apart: 5, of which 3 were waited for; matrix products, arithmetic and copies ran while one was open for 0% of the time, Pallas kernels for 4%

profile of v2, /device:TPU:0, one launch (start us, length us, event | category | flops | bytes accessed | tf_op | source)
XLA Modules:
  0.0 54.5 jit_solution(9645802503339307996)
XLA Ops:
  0.6 1.2 %copy.21 = bf16[4,8,64,128]{3,2,1,0:T(8,128)(2,1)S(1)} copy(bf16[4,8,64,128]{3,1,2,0:T(8,128)(2,1)} %bitcast.55) | data formatting | bytes 1048576
  1.8 0.5 copy.12
  2.3 22.7 %all_to_all.15.got_ref = bf16[32,64,128]{2,1,0:T(8,128)(2,1)S(1)} all-to-all(bf16[32,64,128]{2,1,0:T(8,128)(2,1)S(1)} %bitcast.52), channel_id=1, replica_groups=mesh['dp'=8,'outer'=4] {'dp','outer'}, dimensions={0} | all-to-all | bytes 1048576 | tf_op jit(solution)/shard_map/all_to_all | solution.py:168
  25.1 0.7 %shard_map.109 = (f32[64,128]{1,0:T(8,128)S(1)}, f32[32,1,128]{2,1,0:T(1,128)}) custom-call(bf16[32,64,128]{2,1,0:T(8,128)(2,1)S(1)} %all_to_all.15.got_ref), custom_call_target="tpu_custom_call" | custom-call | tf_op jit(solution)/shard_map/pallas_call | solution.py:131
  25.8 0.0 copy-start
  25.8 0.8 %collective-permute-start.1 = (f32[64,128]{1,0:T(8,128)S(1)}, f32[64,128]{1,0:T(8,128)S(1)}, u32[]{:S(2)}, u32[]{:S(2)}) collective-permute-start(f32[64,128]{1,0:T(8,128)S(1)} %get-tuple-element.18.refs_4_.refs_0_), channel_id=1, source_target_pairs={{0,2},{1,3},{2,0},{3,1},{4,6},{5,7},{6,4},{7,5},{8,10},{9,11},{10,... | collective-permute-start | bytes 98312 | tf_op jit(solution)/shard_map/ppermute | solution.py:152
  26.6 0.1 collective-permute-start
  26.7 3.0 %collective-permute-done.1.refs_6_.refs_2_ = f32[64,128]{1,0:T(8,128)S(1)} collective-permute-done((f32[64,128]{1,0:T(8,128)S(1)}, f32[64,128]{1,0:T(8,128)S(1)}, u32[]{:S(2)}, u32[]{:S(2)}) %collective-permute-start.1) | collective-permute-done | bytes 32800 | tf_op jit(solution)/shard_map/ppermute | solution.py:152
  29.7 0.0 collective-permute-start.2
  29.7 3.1 %all-to-all-start.1 = ((f32[32,1,128]{2,1,0:T(1,128)}), f32[32,1,128]{2,1,0:T(1,128)S(1)}, u32[]{:S(2)}, u32[]{:S(2)}) async-start(f32[32,1,128]{2,1,0:T(1,128)} %get-tuple-element.15), calls=%async_computation.1 | async-start | bytes 32768 | tf_op jit(solution)/shard_map/all_to_all | solution.py:174
  32.8 1.0 %shard_map.110 = (f32[2,128,128]{2,1,0:T(8,128)S(1)}, f32[2,128,128]{2,1,0:T(8,128)S(1)}) custom-call(bf16[2,128,128]{2,1,0:T(8,128)(2,1)} %bitcast.58, bf16[2,128,128]{2,1,0:T(8,128)(2,1)} %bitcast.59, f32[2,2,4]{2,1,0:T(2,128)} %ms_ref.1, f32[2,2,4]{2,1,0:T(2,128)} %vs_ref.1), custom_call_target="tpu_custom_call" | custom-call | tf_op jit(solution)/shard_map/pallas_call | solution.py:131
  33.8 6.1 %all-to-all-done.1.refs_0_.square_ref = f32[32,1,128]{2,1,0:T(1,128)S(1)} async-done(((f32[32,1,128]{2,1,0:T(1,128)}), f32[32,1,128]{2,1,0:T(1,128)S(1)}, u32[]{:S(2)}, u32[]{:S(2)}) %all-to-all-start.1) | async-done | bytes 16416 | tf_op jit(solution)/shard_map/all_to_all | solution.py:174
  39.9 0.0 collective-permute-done.refs_5_.refs_1_
  39.9 0.0 collective-permute-done.2.refs_7_.refs_3_
  39.9 0.0 copy-done
  39.9 0.2 shard_map.112
  40.1 11.6 %all_to_all.16 = bf16[8,128,128]{2,1,0:T(8,128)(2,1)S(1)} all-to-all(bf16[8,128,128]{2,1,0:T(8,128)(2,1)S(1)} %shard_map.112), channel_id=1, replica_groups=mesh['dp'=8,'outer'=4] {'dp'}, dimensions={0} | all-to-all | bytes 524288 | tf_op jit(solution)/shard_map/all_to_all | solution.py:183
  51.8 0.2 copy.24
  52.0 0.1 collective-permute-start.3
  52.1 1.0 %shard_map.111 = (f32[2,128,128]{2,1,0:T(8,128)}, bf16[2,128,128]{2,1,0:T(8,128)(2,1)}, bf16[2,128,128]{2,1,0:T(8,128)(2,1)}, f32[2,2,4]{2,1,0:T(2,128)}, f32[2,2,4]{2,1,0:T(2,128)}) custom-call(f32[32,1,128]{2,1,0:T(1,128)S(1)} %all-to-all-done.1.refs_0_.square_ref, f32[2,128,128]{2,1,0:T(8,128)S(1)} %bitcast.50, ...), custom_call_target="tpu_custom_call" | custom-call | tf_op jit(solution)/shard_map/pallas_call | solution.py:131
  53.1 0.1 stack_reshape.4
  53.2 0.4 collective-permute-done.3
  53.6 0.9 %maximum_select_fusion = bf16[2,16,8192]{2,1,0:T(8,128)(2,1)} fusion(bf16[1,16,8192]{2,1,0:T(8,128)(2,1)S(1)} %bitcast.57, bf16[1,16,8192]{2,1,0:T(8,128)(2,1)S(1)} %stack_reshape.4, pred[]{:T(512)S(6)} %eq.5), kind=kLoop, calls=%fused_computation | loop fusion | flops 786432 | bytes 1048577 | tf_op jit(solution)/shard_map/jit(_where)/select_n | solution.py:192
  (1 shorter events, 0.0 us)
Async XLA Ops:
  25.8 14.1 %copy-start = (f32[2,2,8192]{2,1,0:T(2,128)S(1)}, f32[2,2,8192]{2,1,0:T(2,128)}, u32[]{:S(2)}) copy-start(f32[2,2,8192]{2,1,0:T(2,128)} %param.7) | copy-start | bytes 393220
  25.8 3.9 %collective-permute-start.1 = (f32[64,128]{1,0:T(8,128)S(1)}, f32[64,128]{1,0:T(8,128)S(1)}, u32[]{:S(2)}, u32[]{:S(2)}) collective-permute-start(f32[64,128]{1,0:T(8,128)S(1)} %get-tuple-element.18.refs_4_.refs_0_), channel_id=1, source_target_pairs={{0,2},{1,3},{2,0},{3,1},{4,6},{5,7},{6,4},{7,5},{8,10},{9,11},{10,... | collective-permute-start | bytes 98312 | tf_op jit(solution)/shard_map/ppermute | solution.py:152
  26.6 13.3 %collective-permute-start = (f32[64,128]{1,0:T(8,128)S(1)}, f32[64,128]{1,0:T(8,128)S(1)}, u32[]{:S(2)}, u32[]{:S(2)}) collective-permute-start(f32[64,128]{1,0:T(8,128)S(1)} %get-tuple-element.18.refs_4_.refs_0_), channel_id=1, source_target_pairs={{0,1},{1,0},{2,3},{3,2},{4,5},{5,4},{6,7},{7,6},{8,9},{9,8},{10,11... | collective-permute-start | bytes 98312 | tf_op jit(solution)/shard_map/ppermute | solution.py:152
  29.7 10.2 %collective-permute-start.2 = (f32[64,128]{1,0:T(8,128)S(1)}, f32[64,128]{1,0:T(8,128)S(1)}, u32[]{:S(2)}, u32[]{:S(2)}) collective-permute-start(f32[64,128]{1,0:T(8,128)S(1)} %collective-permute-done.1.refs_6_.refs_2_), channel_id=1, source_target_pairs={{0,1},{1,0},{2,3},{3,2},{4,5},{5,4},{6,7},{7,6},{8,9},{9,8},{10,11... | collective-permute-start | bytes 98312 | tf_op jit(solution)/shard_map/ppermute | solution.py:152
  29.7 10.2 %all-to-all-start.1 = ((f32[32,1,128]{2,1,0:T(1,128)}), f32[32,1,128]{2,1,0:T(1,128)S(1)}, u32[]{:S(2)}, u32[]{:S(2)}) async-start(f32[32,1,128]{2,1,0:T(1,128)} %get-tuple-element.15), calls=%async_computation.1 | async-start | bytes 32768 | tf_op jit(solution)/shard_map/all_to_all | solution.py:174
  52.0 1.6 %collective-permute-start.3 = (bf16[16,8192]{1,0:T(8,128)(2,1)S(1)}, bf16[16,8192]{1,0:T(8,128)(2,1)S(1)}, u32[]{:S(2)}, u32[]{:S(2)}) collective-permute-start(bf16[16,8192]{1,0:T(8,128)(2,1)S(1)} %bitcast.56), channel_id=1, source_target_pairs={{0,1},{1,0},{2,3},{3,2},{4,5},{5,4},{6,7},{7,6},{8,9},{9,8},{10,11... | collective-permute-start | bytes 786440 | tf_op jit(solution)/shard_map/ppermute | solution.py:152

commit v3 on v2

--- a/solution.py
+++ b/solution.py
@@ -13,9 +13,30 @@
 BOTH = ("dp", "outer")
 FIRST_FIX = 1.0 / (1.0 - 0.9**STEP)
 SECOND_FIX = 1.0 / (1.0 - 0.95**STEP)
-
-
-def sum_kernel(got_ref, piece_ref, square_ref):
+SPREAD_EIGHTHS = (2, 7, 6, 1, 0, 5, 3, 4)
+SHARE_EIGHTHS = (2, 3, 0, 4, 5, 6, 1, 7)
+SHARE_QUARTERS = (3, 1, 0, 2)
+
+
+def ordered(size, parts):
+    if size % len(parts):
+        return list(range(size))
+    span = size // len(parts)
+    return [part * span + i for part in parts for i in range(span)]
+
+
+def arrange(value, parts):
+    if value.shape[0] % len(parts):
+        return value
+    blocks = jnp.split(value, len(parts), axis=0)
+    return jnp.concatenate([blocks[part] for part in parts], axis=0)
+
+
+def inverse(parts):
+    return tuple(parts.index(i) for i in range(len(parts)))
+
+
+def sum_kernel(count, rows, got_ref, piece_ref, square_ref):
     terms = got_ref.shape[0]
     group = 8
 
@@ -28,7 +49,11 @@
             total = total + some(i)
     else:
         total = lax.fori_loop(1, terms // group, lambda i, held: held + some(i), total)
-    piece_ref[...] = total
+    part = total.shape[0] // (count * rows)
+    for at in range(count):
+        for row in range(rows):
+            start = (at * rows + row) * part
+            piece_ref[pl.ds(at * rows * part + row, part, stride=rows), :] = total[start : start + part]
     lanes = jnp.sum(total * total, axis=0, keepdims=True)
     square_ref[...] = jnp.broadcast_to(lanes[None], square_ref.shape)
 
@@ -63,8 +88,8 @@
     return master_ref[at, here, :] - 0.01 * update
 
 
-def weight_kernel(square_ref, master_ref, m_ref, v_ref, *refs):
-    *piece_refs, out_ref = refs
+def weight_kernel(rows, square_ref, master_ref, m_ref, v_ref, *refs):
+    *piece_refs, out_ref, hold_ref = refs
     outer_at = lax.axis_index("outer")
     side = outer_at % 2
     held = piece_refs[0].shape[0] // master_ref.shape[0]
@@ -73,8 +98,29 @@
         here = pl.ds(pl.multiple_of((outer_at ^ offset) * held, SUBLANES), held)
         start = pl.multiple_of(side * held, SUBLANES)
         m, v = moments(clip, piece_ref, m_ref, v_ref, side, start, here, held)
-        fresh = fresh_of(master_ref, side, here, m, v).astype(jnp.bfloat16)
-        out_ref[:, here, :] = jnp.broadcast_to(fresh[None], (out_ref.shape[0],) + fresh.shape)
+        hold_ref[offset] = fresh_of(master_ref, side, here, m, v)
+        part = held // rows
+        for row in range(rows):
+            fresh = hold_ref[offset, pl.ds(row, part, stride=rows), :].astype(jnp.bfloat16)
+            start = row * (out_ref.shape[1] // rows) + (outer_at ^ offset) * part
+            there = pl.ds(pl.multiple_of(start, SUBLANES), part)
+            out_ref[:, there, :] = jnp.broadcast_to(fresh[None], (out_ref.shape[0],) + fresh.shape)
+
+
+def half_copy(half_ref, weights_ref, side, sem):
+    return pltpu.make_async_copy(half_ref, weights_ref.at[side], sem)
+
+
+def halves_kernel(mine_ref, other_ref, out_ref, sems):
+    side = lax.axis_index("outer") % 2
+    copies = [
+        half_copy(mine_ref, out_ref, side, sems.at[0]),
+        half_copy(other_ref, out_ref, 1 - side, sems.at[1]),
+    ]
+    for copy in copies:
+        copy.start()
+    for copy in copies:
+        copy.wait()
 
 
 def state_kernel(rows, square_ref, master_ref, m_ref, v_ref, *refs):
@@ -115,25 +161,28 @@
         v_top_ref[at] = v_tops
 
 
+def is_small(value):
+    return value.size * value.dtype.itemsize <= NEAR_BYTES
+
+
 def near(value):
-    if value.size * value.dtype.itemsize > NEAR_BYTES:
-        return value
-    return pltpu.with_memory_space_constraint(value, pltpu.VMEM)
-
-
-def call(kernel, outs, args, near_in=True, near_out=True):
-    def shape_of(shape, dtype):
-        plain_shape = jax.ShapeDtypeStruct(shape, dtype)
-        small = plain_shape.size * plain_shape.dtype.itemsize <= NEAR_BYTES
-        return pltpu.VMEM(shape, dtype) if near_out and small else plain_shape
-
+    return pltpu.with_memory_space_constraint(value, pltpu.VMEM) if is_small(value) else value
+
+
+def call(kernel, outs, args, in_specs=None, out_specs=None, **extra):
     spec = pl.BlockSpec(memory_space=pltpu.VMEM)
     return pl.pallas_call(
         kernel,
-        out_shape=[shape_of(*out) for out in outs],
-        in_specs=[spec] * len(args),
-        out_specs=[spec] * len(outs),
-    )(*[near(a) if near_in else a for a in args])
+        out_shape=outs,
+        in_specs=in_specs or [spec] * len(args),
+        out_specs=out_specs or [spec] * len(outs),
+        **extra,
+    )(*args)
+
+
+def near_shape(shape, dtype):
+    far = jax.ShapeDtypeStruct(shape, dtype)
+    return pltpu.VMEM(shape, dtype) if is_small(far) else far
 
 
 def dense(value):
@@ -163,14 +212,24 @@
         tiles = width // LANES
         part = tiles // outer_n
         tall = (count, tiles * rows, LANES)
+        vmem, far = pl.BlockSpec(memory_space=pltpu.VMEM), pl.BlockSpec(memory_space=pl.ANY)
+        shape_of = jax.ShapeDtypeStruct
         pieces = own.reshape(count, dp_n, rows, outer_n, part, LANES)
-        pieces = pieces.transpose(1, 3, 0, 4, 2, 5).reshape(total_n, count * part * rows, LANES)
-        got = lax.all_to_all(pieces, BOTH, 0, 0, tiled=True)
+        pieces = arrange(pieces.transpose(1, 3, 0, 2, 4, 5), SHARE_EIGHTHS)
+        pieces = arrange(pieces.transpose(1, 0, 2, 3, 4, 5), SHARE_QUARTERS)
+        pieces = pieces.reshape(total_n, count * rows * part, LANES)
+        share_dp, share_outer = ordered(dp_n, SHARE_EIGHTHS), ordered(outer_n, SHARE_QUARTERS)
+        share = [d * outer_n + o for o in share_outer for d in share_dp]
+        got = lax.all_to_all(pieces, BOTH, 0, 0, axis_index_groups=[share], tiled=True)
         m_part, v_part = call(
-            prep_kernel, [(tall, f32), (tall, f32)],
-            [dense(m_codes), dense(v_codes), m_scales, v_scales], near_in=False,
-        )
-        piece, square = call(sum_kernel, [(got.shape[1:], f32), ((total_n, 1, LANES), f32)], [got])
+            prep_kernel, [near_shape(tall, f32)] * 2,
+            [dense(m_codes), dense(v_codes), m_scales, v_scales],
+        )
+        piece, square = call(
+            lambda *refs: sum_kernel(count, rows, *refs),
+            [near_shape(got.shape[1:], f32), shape_of((total_n, 1, LANES), f32)],
+            [near(got)],
+        )
         squares = lax.all_to_all(square, BOTH, 0, 0, tiled=True)
         held = {0: piece}
         bit = outer_n // 2
@@ -179,17 +238,30 @@
                 held[at ^ bit] = flip(held[at], outer_n, bit)
             bit //= 2
         args = [squares, dense(master), m_part, v_part] + [held[i] for i in range(outer_n)]
-        (mine,) = call(weight_kernel, [((dp_n, tiles * rows, LANES), bf16)], args)
-        mine = lax.all_to_all(mine, "dp", 0, 0, tiled=True)
+        args = [near(a) for a in args]
+        (mine,) = call(
+            lambda *refs: weight_kernel(rows, *refs),
+            [near_shape((dp_n, rows * tiles, LANES), bf16)], args,
+            scratch_shapes=[pltpu.VMEM((outer_n, part * rows, LANES), f32)],
+        )
+        spread = ordered(dp_n, SPREAD_EIGHTHS)
+        mine = lax.all_to_all(mine, "dp", 0, 0, axis_index_groups=[spread], tiled=True)
+        mine = arrange(mine, inverse(SPREAD_EIGHTHS)).reshape(rows_all, width)
+        half_spec = vmem if is_small(mine) else far
+        other = flip(mine, outer_n, 1)
         fresh, m_next, v_next, m_top, v_top = call(
             lambda *refs: state_kernel(rows, *refs),
-            [(tall, f32), (tall, bf16), (tall, bf16), (m_scales.shape, f32), (v_scales.shape, f32)],
-            args, near_out=False,
-        )
-        mine = mine.reshape(dp_n, tiles, rows, LANES).transpose(0, 2, 1, 3).reshape(rows_all, width)
-        other = flip(mine, outer_n, 1)
-        side = lax.axis_index("outer") % 2
-        weights = jnp.where(side == 0, jnp.stack([mine, other]), jnp.stack([other, mine]))
+            [
+                shape_of(tall, f32), shape_of(tall, bf16), shape_of(tall, bf16),
+                shape_of(m_scales.shape, f32), shape_of(v_scales.shape, f32),
+            ],
+            args,
+        )
+        (weights,) = call(
+            halves_kernel, [shape_of(own.shape, bf16)], [near(mine), near(other)],
+            in_specs=[half_spec] * 2, out_specs=[far],
+            scratch_shapes=[pltpu.SemaphoreType.DMA((2,))],
+        )
         return (plain(fresh, rows), plain(m_next, rows), plain(v_next, rows), m_top, v_top, weights)
 
     return body

time: 54.7 us -> 51.6 us (0.943)
  blocking collectives: 34.4 us -> 31.5 us
  Pallas kernels: 2.82 us -> 3.64 us
  other arithmetic: 0.87 us -> 0.07 us
    all_to_all x2, blocking collectives: 34.4 us -> 31.5 us  [the longest x1 21.8 us: body(): lax.all_to_all(pieces, BOTH, 0, 0, axis_index_groups=[share], tiled=True)]
    select_n x1 -> x0, other arithmetic: 0.87 us -> none  [body(): jnp.where(side == 0, jnp.stack([mine, other]), jnp.stack([other, mine]))]
    pallas_call x4 -> x5, Pallas kernels: 2.82 us -> 3.64 us  [call(): pl.pallas_call(kernel, out_shape=outs, in_specs=in_specs or [spec] * len(...]
    unnamed x4 -> x13, local copies, waits for them, and re-layouts: 1.33 us -> 1.29 us
where the time goes in v3:
time: 51.6 us; the launch traced here: 51.3 us
  blocking collectives  31.5 us (61%)
  waiting for transfers between devices  9.36 us (18%)
  starting transfers between devices  4.45 us (9%)
  Pallas kernels  3.64 us (7%)
  local copies, waits for them, and re-layouts  1.52 us (3%)
  between operations  0.76 us (1%)
    all_to_all x1, blocking collectives, body(): lax.all_to_all(pieces, BOTH, 0, 0, axis_index_groups=[share], tiled=True)  21.8 us
    all_to_all x1, blocking collectives, body(): lax.all_to_all(mine, 'dp', 0, 0, axis_index_groups=[spread], tiled=True)  9.65 us
    all_to_all x1, waiting for transfers between devices, body(): squares = lax.all_to_all(square, BOTH, 0, 0, tiled=True)  6.12 us
    pallas_call x5, Pallas kernels, call(): pl.pallas_call(kernel, out_shape=outs, in_specs=in_specs or [spec] * len(...  3.64 us
    ppermute x4, waiting for transfers between devices, flip(): return lax.ppermute(value, 'outer', [(i, i ^ bit) for i in range(size)])  3.23 us
    all_to_all x1, starting transfers between devices, body(): squares = lax.all_to_all(square, BOTH, 0, 0, tiled=True)  3.15 us
    ppermute x4, starting transfers between devices, flip(): return lax.ppermute(value, 'outer', [(i, i ^ bit) for i in range(size)])  1.3 us
    unnamed x13, local copies, waits for them, and re-layouts  1.29 us
  transfers between devices with their start and end apart: 5, of which 3 were waited for; matrix products, arithmetic and copies ran while one was open for 0% of the time, Pallas kernels for 4%

profile of v3, /device:TPU:0, one launch (start us, length us, event | category | flops | bytes accessed | tf_op | source)
XLA Modules:
  0.0 51.3 jit_solution(1005774649521965586)
XLA Ops:
  0.6 1.2 %copy.19 = bf16[4,8,64,128]{3,2,1,0:T(8,128)(2,1)S(1)} copy(bf16[4,8,64,128]{3,1,2,0:T(8,128)(2,1)} %bitcast.50) | data formatting | bytes 1048576
  1.8 0.1 copy.21
  2.0 0.1 pad_maximum_fusion
  2.1 21.8 %all_to_all.15.refs_0_ = bf16[32,64,128]{2,1,0:T(8,128)(2,1)S(1)} all-to-all(bf16[32,64,128]{2,1,0:T(8,128)(2,1)S(1)} %bitcast.47), channel_id=1, replica_groups={{11,15,3,19,23,27,7,31,9,13,1,17,21,25,5,29,8,12,0,16,20,24,4,28,10,14,..., dimensions={0} | all-to-all | bytes 1048576 | tf_op jit(solution)/shard_map/all_to_all | solution.py:223
  23.9 0.7 %shard_map.109 = (f32[64,128]{1,0:T(8,128)S(1)}, f32[32,1,128]{2,1,0:T(1,128)}) custom-call(bf16[32,64,128]{2,1,0:T(8,128)(2,1)S(1)} %all_to_all.15.refs_0_), custom_call_target="tpu_custom_call" | custom-call | tf_op jit(solution)/shard_map/pallas_call | solution.py:174
  24.6 0.0 copy-start
  24.6 1.2 %collective-permute-start.1 = (f32[64,128]{1,0:T(8,128)S(1)}, f32[64,128]{1,0:T(8,128)S(1)}, u32[]{:S(2)}, u32[]{:S(2)}) collective-permute-start(f32[64,128]{1,0:T(8,128)S(1)} %get-tuple-element.18.refs_4_), channel_id=1, source_target_pairs={{0,2},{1,3},{2,0},{3,1},{4,6},{5,7},{6,4},{7,5},{8,10},{9,11},{10,... | collective-permute-start | bytes 98312 | tf_op jit(solution)/shard_map/ppermute | solution.py:201
  25.9 0.0 collective-permute-start
  25.9 2.7 %collective-permute-done.1.refs_6_ = f32[64,128]{1,0:T(8,128)S(1)} collective-permute-done((f32[64,128]{1,0:T(8,128)S(1)}, f32[64,128]{1,0:T(8,128)S(1)}, u32[]{:S(2)}, u32[]{:S(2)}) %collective-permute-start.1) | collective-permute-done | bytes 32800 | tf_op jit(solution)/shard_map/ppermute | solution.py:201
  28.5 0.0 collective-permute-start.2
  28.5 3.1 %all-to-all-start.1 = ((f32[32,1,128]{2,1,0:T(1,128)}), f32[32,1,128]{2,1,0:T(1,128)S(1)}, u32[]{:S(2)}, u32[]{:S(2)}) async-start(f32[32,1,128]{2,1,0:T(1,128)} %get-tuple-element.15), calls=%async_computation.1 | async-start | bytes 32768 | tf_op jit(solution)/shard_map/all_to_all | solution.py:233
  31.7 1.0 %shard_map.110 = (f32[2,128,128]{2,1,0:T(8,128)S(1)}, f32[2,128,128]{2,1,0:T(8,128)S(1)}) custom-call(bf16[2,128,128]{2,1,0:T(8,128)(2,1)} %bitcast.51, bf16[2,128,128]{2,1,0:T(8,128)(2,1)} %bitcast.52, f32[2,2,4]{2,1,0:T(2,128)} %ms_ref.1, f32[2,2,4]{2,1,0:T(2,128)} %vs_ref.1), custom_call_target="tpu_custom_call" | custom-call | tf_op jit(solution)/shard_map/pallas_call | solution.py:174
  32.7 6.1 %all-to-all-done.1.refs_0_ = f32[32,1,128]{2,1,0:T(1,128)S(1)} async-done(((f32[32,1,128]{2,1,0:T(1,128)}), f32[32,1,128]{2,1,0:T(1,128)S(1)}, u32[]{:S(2)}, u32[]{:S(2)}) %all-to-all-start.1) | async-done | bytes 16416 | tf_op jit(solution)/shard_map/all_to_all | solution.py:233
  38.8 0.0 collective-permute-done.refs_5_
  38.8 0.0 collective-permute-done.2.refs_7_
  38.8 0.0 copy-done
  38.8 0.2 shard_map.112
  39.0 9.6 %all_to_all.16 = bf16[8,128,128]{2,1,0:T(8,128)(2,1)S(1)} all-to-all(bf16[8,128,128]{2,1,0:T(8,128)(2,1)S(1)} %shard_map.112), channel_id=1, replica_groups={{8,28,24,4,0,20,12,16},{9,29,25,5,1,21,13,17},{10,30,26,6,2,22,14,18},{..., dimensions={0} | all-to-all | bytes 524288 | tf_op jit(solution)/shard_map/all_to_all | solution.py:248
  48.8 0.1 reshape.67.mine_ref
  48.9 0.1 collective-permute-start.3
  49.0 1.0 %shard_map.111 = (f32[2,128,128]{2,1,0:T(8,128)}, bf16[2,128,128]{2,1,0:T(8,128)(2,1)}, bf16[2,128,128]{2,1,0:T(8,128)(2,1)}, f32[2,2,4]{2,1,0:T(2,128)}, f32[2,2,4]{2,1,0:T(2,128)}) custom-call(f32[32,1,128]{2,1,0:T(1,128)S(1)} %all-to-all-done.1.refs_0_, f32[2,128,128]{2,1,0:T(8,128)S(1)} %bitcast.41, f32[2,128,128]{2,1,0:T(8,128)S(1)} %get-tuple-element.16.refs_2_, ...), custom_call_target="tpu_custom_call" | custom-call | tf_op jit(solution)/shard_map/pallas_call | solution.py:174
  49.9 0.5 %collective-permute-done.3.other_ref = bf16[16,8192]{1,0:T(8,128)(2,1)S(1)} collective-permute-done((bf16[16,8192]{1,0:T(8,128)(2,1)S(1)}, bf16[16,8192]{1,0:T(8,128)(2,1)S(1)}, u32[]{:S(2)}, u32[]{:S(2)}) %collective-permute-start.3) | collective-permute-done | bytes 262176 | tf_op jit(solution)/shard_map/ppermute | solution.py:201
  50.5 0.8 %shard_map.113 = bf16[2,16,8192]{2,1,0:T(8,128)(2,1)} custom-call(bf16[16,8192]{1,0:T(8,128)(2,1)S(1)} %reshape.67.mine_ref, bf16[16,8192]{1,0:T(8,128)(2,1)S(1)} %collective-permute-done.3.other_ref), custom_call_target="tpu_custom_call" | custom-call | tf_op jit(solution)/shard_map/pallas_call | solution.py:174
  (13 shorter events, 0.2 us)
Async XLA Ops:
  24.6 14.2 %copy-start = (f32[2,2,8192]{2,1,0:T(2,128)S(1)}, f32[2,2,8192]{2,1,0:T(2,128)}, u32[]{:S(2)}) copy-start(f32[2,2,8192]{2,1,0:T(2,128)} %param.7) | copy-start | bytes 393220
  24.6 3.9 %collective-permute-start.1 = (f32[64,128]{1,0:T(8,128)S(1)}, f32[64,128]{1,0:T(8,128)S(1)}, u32[]{:S(2)}, u32[]{:S(2)}) collective-permute-start(f32[64,128]{1,0:T(8,128)S(1)} %get-tuple-element.18.refs_4_), channel_id=1, source_target_pairs={{0,2},{1,3},{2,0},{3,1},{4,6},{5,7},{6,4},{7,5},{8,10},{9,11},{10,... | collective-permute-start | bytes 98312 | tf_op jit(solution)/shard_map/ppermute | solution.py:201
  25.9 13.0 %collective-permute-start = (f32[64,128]{1,0:T(8,128)S(1)}, f32[64,128]{1,0:T(8,128)S(1)}, u32[]{:S(2)}, u32[]{:S(2)}) collective-permute-start(f32[64,128]{1,0:T(8,128)S(1)} %get-tuple-element.18.refs_4_), channel_id=1, source_target_pairs={{0,1},{1,0},{2,3},{3,2},{4,5},{5,4},{6,7},{7,6},{8,9},{9,8},{10,11... | collective-permute-start | bytes 98312 | tf_op jit(solution)/shard_map/ppermute | solution.py:201
  28.5 10.3 %collective-permute-start.2 = (f32[64,128]{1,0:T(8,128)S(1)}, f32[64,128]{1,0:T(8,128)S(1)}, u32[]{:S(2)}, u32[]{:S(2)}) collective-permute-start(f32[64,128]{1,0:T(8,128)S(1)} %collective-permute-done.1.refs_6_), channel_id=1, source_target_pairs={{0,1},{1,0},{2,3},{3,2},{4,5},{5,4},{6,7},{7,6},{8,9},{9,8},{10,11... | collective-permute-start | bytes 98312 | tf_op jit(solution)/shard_map/ppermute | solution.py:201
  28.5 10.3 %all-to-all-start.1 = ((f32[32,1,128]{2,1,0:T(1,128)}), f32[32,1,128]{2,1,0:T(1,128)S(1)}, u32[]{:S(2)}, u32[]{:S(2)}) async-start(f32[32,1,128]{2,1,0:T(1,128)} %get-tuple-element.15), calls=%async_computation.1 | async-start | bytes 32768 | tf_op jit(solution)/shard_map/all_to_all | solution.py:233
  48.9 1.6 %collective-permute-start.3 = (bf16[16,8192]{1,0:T(8,128)(2,1)S(1)}, bf16[16,8192]{1,0:T(8,128)(2,1)S(1)}, u32[]{:S(2)}, u32[]{:S(2)}) collective-permute-start(bf16[16,8192]{1,0:T(8,128)(2,1)S(1)} %reshape.67.mine_ref), channel_id=1, source_target_pairs={{0,1},{1,0},{2,3},{3,2},{4,5},{5,4},{6,7},{7,6},{8,9},{9,8},{10,11... | collective-permute-start | bytes 786440 | tf_op jit(solution)/shard_map/ppermute | solution.py:201

commit v4 on v3

--- a/solution.py
+++ b/solution.py
@@ -36,7 +36,15 @@
     return tuple(parts.index(i) for i in range(len(parts)))
 
 
-def sum_kernel(count, rows, got_ref, piece_ref, square_ref):
+def sum_kernel(got_ref, v_ref, ms_ref, vs_ref, piece_ref, square_ref, scale_ref, v_out_ref):
+    count, rows, blocks = ms_ref.shape
+    span = BLOCK // LANES * rows
+    for at in range(count):
+        for block in range(blocks):
+            here = pl.ds(block * span, span)
+            v_out_ref[at, here, :] = 0.95 * scaled_rows(v_ref[at, here, :], scale_rows(vs_ref, at, block, rows))
+            wide = jnp.broadcast_to(scale_rows(ms_ref, at, block, rows), (SUBLANES, LANES))
+            scale_ref[at, block] = wide
     terms = got_ref.shape[0]
     group = 8
 
@@ -58,19 +66,14 @@
     square_ref[...] = jnp.broadcast_to(lanes[None], square_ref.shape)
 
 
-def prep_kernel(m_ref, v_ref, ms_ref, vs_ref, m_out_ref, v_out_ref):
-    count, rows, blocks = ms_ref.shape
-    span = BLOCK // LANES * rows
-    for at in range(count):
-        for block in range(blocks):
-            here = pl.ds(block * span, span)
-            for code_ref, scale_ref, decay, out_ref in (
-                (m_ref, ms_ref, 0.9, m_out_ref),
-                (v_ref, vs_ref, 0.95, v_out_ref),
-            ):
-                scale = scale_ref[at, :, block : block + 1]
-                scale = jnp.concatenate([scale] * (span // rows), axis=0)
-                out_ref[at, here, :] = decay * (code_ref[at, here, :].astype(jnp.float32) * scale)
+def scale_rows(scale_ref, at, block, rows):
+    scale = scale_ref[at, :, block : block + 1]
+    return jnp.concatenate([scale] * (SUBLANES // rows), axis=0)
+
+
+def scaled_rows(codes, scale):
+    tiles = codes.astype(jnp.float32).reshape(codes.shape[0] // SUBLANES, SUBLANES, LANES)
+    return (tiles * scale).reshape(codes.shape)
 
 
 def clip_of(square_ref):
@@ -78,9 +81,11 @@
     return 1.0 / jnp.maximum(jnp.sqrt(total), 1.0)
 
 
-def moments(clip, piece_ref, m_ref, v_ref, at, start, here, span):
+def moments(clip, piece_ref, m_ref, scale_ref, v_ref, at, start, block, span):
+    here = pl.ds(pl.multiple_of(block * span, SUBLANES), span)
     g = clip * piece_ref[pl.ds(start, span), :]
-    return m_ref[at, here, :] + 0.1 * g, v_ref[at, here, :] + 0.05 * g * g
+    m = 0.9 * scaled_rows(m_ref[at, here, :], scale_ref[at, block]) + 0.1 * g
+    return m, v_ref[at, here, :] + 0.05 * g * g, here
 
 
 def fresh_of(master_ref, at, here, m, v):
@@ -88,23 +93,25 @@
     return master_ref[at, here, :] - 0.01 * update
 
 
-def weight_kernel(rows, square_ref, master_ref, m_ref, v_ref, *refs):
+def weight_kernel(rows, square_ref, master_ref, m_ref, scale_ref, v_ref, *refs):
     *piece_refs, out_ref, hold_ref = refs
     outer_at = lax.axis_index("outer")
     side = outer_at % 2
     held = piece_refs[0].shape[0] // master_ref.shape[0]
+    span = BLOCK // LANES * rows
+    part = span // rows
     clip = clip_of(square_ref)
     for offset, piece_ref in enumerate(piece_refs):
-        here = pl.ds(pl.multiple_of((outer_at ^ offset) * held, SUBLANES), held)
-        start = pl.multiple_of(side * held, SUBLANES)
-        m, v = moments(clip, piece_ref, m_ref, v_ref, side, start, here, held)
-        hold_ref[offset] = fresh_of(master_ref, side, here, m, v)
-        part = held // rows
-        for row in range(rows):
-            fresh = hold_ref[offset, pl.ds(row, part, stride=rows), :].astype(jnp.bfloat16)
-            start = row * (out_ref.shape[1] // rows) + (outer_at ^ offset) * part
-            there = pl.ds(pl.multiple_of(start, SUBLANES), part)
-            out_ref[:, there, :] = jnp.broadcast_to(fresh[None], (out_ref.shape[0],) + fresh.shape)
+        for inner in range(held // span):
+            block = (outer_at ^ offset) * (held // span) + inner
+            start = pl.multiple_of(side * held + inner * span, SUBLANES)
+            m, v, here = moments(clip, piece_ref, m_ref, scale_ref, v_ref, side, start, block, span)
+            hold_ref[offset, inner] = fresh_of(master_ref, side, here, m, v)
+            for row in range(rows):
+                fresh = hold_ref[offset, inner, pl.ds(row, part, stride=rows), :].astype(jnp.bfloat16)
+                at = row * (out_ref.shape[1] // rows) + block * part
+                there = pl.ds(pl.multiple_of(at, SUBLANES), part)
+                out_ref[:, there, :] = jnp.broadcast_to(fresh[None], (out_ref.shape[0],) + fresh.shape)
 
 
 def half_copy(half_ref, weights_ref, side, sem):
@@ -123,7 +130,7 @@
         copy.wait()
 
 
-def state_kernel(rows, square_ref, master_ref, m_ref, v_ref, *refs):
+def state_kernel(rows, square_ref, master_ref, m_ref, scale_ref, v_ref, *refs):
     *piece_refs, fresh_ref, m_next_ref, v_next_ref, m_top_ref, v_top_ref = refs
     outer_at = lax.axis_index("outer")
     count = master_ref.shape[0]
@@ -149,8 +156,8 @@
         for offset, piece_ref in enumerate(piece_refs):
             for inner in range(held // span):
                 block = (outer_at ^ offset) * (held // span) + inner
-                here = pl.ds(pl.multiple_of(block * span, SUBLANES), span)
-                m, v = moments(clip, piece_ref, m_ref, v_ref, at, at * held + inner * span, here, span)
+                start = at * held + inner * span
+                m, v, here = moments(clip, piece_ref, m_ref, scale_ref, v_ref, at, start, block, span)
                 fresh_ref[at, here, :] = fresh_of(master_ref, at, here, m, v)
                 m_top, v_top = top_of(m), top_of(v)
                 m_next_ref[at, here, :] = scaled(m, m_top)
@@ -221,28 +228,25 @@
         share_dp, share_outer = ordered(dp_n, SHARE_EIGHTHS), ordered(outer_n, SHARE_QUARTERS)
         share = [d * outer_n + o for o in share_outer for d in share_dp]
         got = lax.all_to_all(pieces, BOTH, 0, 0, axis_index_groups=[share], tiled=True)
-        m_part, v_part = call(
-            prep_kernel, [near_shape(tall, f32)] * 2,
-            [dense(m_codes), dense(v_codes), m_scales, v_scales],
-        )
-        piece, square = call(
-            lambda *refs: sum_kernel(count, rows, *refs),
-            [near_shape(got.shape[1:], f32), shape_of((total_n, 1, LANES), f32)],
-            [near(got)],
+        blocks = m_scales.shape[2]
+        piece, square, scales, v_part = call(
+            sum_kernel,
+            [
+                near_shape(got.shape[1:], f32), shape_of((total_n, 1, LANES), f32),
+                near_shape((count, blocks, SUBLANES, LANES), f32), near_shape(tall, f32),
+            ],
+            [near(a) for a in (got, dense(v_codes), m_scales, v_scales)],
         )
         squares = lax.all_to_all(square, BOTH, 0, 0, tiled=True)
         held = {0: piece}
-        bit = outer_n // 2
-        while bit:
-            for at in list(held):
-                held[at ^ bit] = flip(held[at], outer_n, bit)
-            bit //= 2
-        args = [squares, dense(master), m_part, v_part] + [held[i] for i in range(outer_n)]
+        for at in range(outer_n - 1, 0, -1):
+            held[at] = flip(piece, outer_n, at)
+        args = [squares, dense(master), dense(m_codes), scales, v_part] + [held[i] for i in range(outer_n)]
         args = [near(a) for a in args]
         (mine,) = call(
             lambda *refs: weight_kernel(rows, *refs),
             [near_shape((dp_n, rows * tiles, LANES), bf16)], args,
-            scratch_shapes=[pltpu.VMEM((outer_n, part * rows, LANES), f32)],
+            scratch_shapes=[pltpu.VMEM((outer_n, blocks // outer_n, tiles // blocks * rows, LANES), f32)],
         )
         spread = ordered(dp_n, SPREAD_EIGHTHS)
         mine = lax.all_to_all(mine, "dp", 0, 0, axis_index_groups=[spread], tiled=True)

time: 51.6 us -> 49.5 us (0.959)
  blocking collectives: 31.5 us -> 41.6 us
  waiting for transfers between devices: 9.36 us -> 0.54 us
  starting transfers between devices: 4.45 us -> 1.93 us
  Pallas kernels: 3.64 us -> 2.72 us
    all_to_all x0 -> x1, blocking collectives: none -> 10.1 us  [body(): squares = lax.all_to_all(square, BOTH, 0, 0, tiled=True)]
    all_to_all x1 -> x0, waiting for transfers between devices: 6.12 us -> none  [body(): squares = lax.all_to_all(square, BOTH, 0, 0, tiled=True)]
    all_to_all x1 -> x0, starting transfers between devices: 3.15 us -> none  [body(): squares = lax.all_to_all(square, BOTH, 0, 0, tiled=True)]
    ppermute x4, waiting for transfers between devices: 3.23 us -> 0.54 us  [flip(): return lax.ppermute(value, 'outer', [(i, i ^ bit) for i in range(size)])]
    pallas_call x5 -> x4, Pallas kernels: 3.64 us -> 2.72 us  [call(): pl.pallas_call(kernel, out_shape=outs, in_specs=in_specs or [spec] * len(...]
    ppermute x4, starting transfers between devices: 1.3 us -> 1.93 us  [flip(): return lax.ppermute(value, 'outer', [(i, i ^ bit) for i in range(size)])]
    unnamed x13 -> x21, local copies, waits for them, and re-layouts: 1.29 us -> 1.32 us
  transfers between devices with their start and end apart: 5 -> 4, of which waited for: 3 -> 1; matrix products, arithmetic and copies ran while one was open for 0% -> 0% of each run, Pallas kernels for 4% -> 2%
where the time goes in v4:
time: 49.5 us; the launch traced here: 49.2 us
  blocking collectives  41.6 us (84%)
  Pallas kernels  2.72 us (5%)
  starting transfers between devices  1.93 us (4%)
  local copies, waits for them, and re-layouts  1.55 us (3%)
  between operations  0.81 us (2%)
  waiting for transfers between devices  0.54 us (1%)
    all_to_all x1, blocking collectives, body(): lax.all_to_all(pieces, BOTH, 0, 0, axis_index_groups=[share], tiled=True)  21.8 us
    all_to_all x1, blocking collectives, body(): squares = lax.all_to_all(square, BOTH, 0, 0, tiled=True)  10.1 us
    all_to_all x1, blocking collectives, body(): lax.all_to_all(mine, 'dp', 0, 0, axis_index_groups=[spread], tiled=True)  9.65 us
    pallas_call x4, Pallas kernels, call(): pl.pallas_call(kernel, out_shape=outs, in_specs=in_specs or [spec] * len(...  2.72 us
    ppermute x4, starting transfers between devices, flip(): return lax.ppermute(value, 'outer', [(i, i ^ bit) for i in range(size)])  1.93 us
    unnamed x21, local copies, waits for them, and re-layouts  1.32 us
  transfers between devices with their start and end apart: 4, of which 1 were waited for; matrix products, arithmetic and copies ran while one was open for 0% of the time, Pallas kernels for 2%

profile of v4, /device:TPU:0, one launch (start us, length us, event | category | flops | bytes accessed | tf_op | source)
XLA Modules:
  0.0 49.2 jit_solution(2009902367760305024)
XLA Ops:
  0.6 1.2 %copy.19 = bf16[4,8,64,128]{3,2,1,0:T(8,128)(2,1)S(1)} copy(bf16[4,8,64,128]{3,1,2,0:T(8,128)(2,1)} %bitcast.53) | data formatting | bytes 1048576
  1.8 0.1 copy.21
  2.0 0.1 pad_maximum_fusion
  2.1 0.0 copy-start.2
  2.1 0.0 copy-start.3
  2.1 0.0 copy-start.4
  2.1 21.8 %all_to_all.15.got_ref = bf16[32,64,128]{2,1,0:T(8,128)(2,1)S(1)} all-to-all(bf16[32,64,128]{2,1,0:T(8,128)(2,1)S(1)} %bitcast.50), channel_id=1, replica_groups={{11,15,3,19,23,27,7,31,9,13,1,17,21,25,5,29,8,12,0,16,20,24,4,28,10,14,..., dimensions={0} | all-to-all | bytes 1048576 | tf_op jit(solution)/shard_map/all_to_all | solution.py:230
  24.0 0.0 copy-start
  24.0 0.0 copy-start.1
  24.0 0.7 %shard_map.109 = (f32[64,128]{1,0:T(8,128)S(1)}, f32[32,1,128]{2,1,0:T(1,128)}, f32[2,4,8,128]{3,2,1,0:T(8,128)S(1)}, f32[2,128,128]{2,1,0:T(8,128)S(1)}) custom-call(bf16[32,64,128]{2,1,0:T(8,128)(2,1)S(1)} %all_to_all.15.got_ref, bf16[2,128,128]{2,1,0:T(8,128)(2,1)S(1)} %bitcast.44, f32[2,2,4]{2,1,0:T(2,128)S(1)} %copy-done.3, f32[2,2,4]{2,1,0:T(2,128)S(1)} %copy-done.4), custom_call_target="tpu_custom_call" | custom-call | tf_op jit(solution)/shard_map/pallas_call | solution.py:181
  24.7 0.5 %collective-permute-start.2 = (f32[64,128]{1,0:T(8,128)S(1)}, f32[64,128]{1,0:T(8,128)S(1)}, u32[]{:S(2)}, u32[]{:S(2)}) collective-permute-start(f32[64,128]{1,0:T(8,128)S(1)} %get-tuple-element.18.refs_5_), channel_id=1, source_target_pairs={{0,3},{1,2},{2,1},{3,0},{4,7},{5,6},{6,5},{7,4},{8,11},{9,10},{10,... | collective-permute-start | bytes 98312 | tf_op jit(solution)/shard_map/ppermute | solution.py:208
  25.2 0.7 %collective-permute-start.1 = (f32[64,128]{1,0:T(8,128)S(1)}, f32[64,128]{1,0:T(8,128)S(1)}, u32[]{:S(2)}, u32[]{:S(2)}) collective-permute-start(f32[64,128]{1,0:T(8,128)S(1)} %get-tuple-element.18.refs_5_), channel_id=1, source_target_pairs={{0,2},{1,3},{2,0},{3,1},{4,6},{5,7},{6,4},{7,5},{8,10},{9,11},{10,... | collective-permute-start | bytes 98312 | tf_op jit(solution)/shard_map/ppermute | solution.py:208
  26.0 0.6 %collective-permute-start = (f32[64,128]{1,0:T(8,128)S(1)}, f32[64,128]{1,0:T(8,128)S(1)}, u32[]{:S(2)}, u32[]{:S(2)}) collective-permute-start(f32[64,128]{1,0:T(8,128)S(1)} %get-tuple-element.18.refs_5_), channel_id=1, source_target_pairs={{0,1},{1,0},{2,3},{3,2},{4,5},{5,4},{6,7},{7,6},{8,9},{9,8},{10,11... | collective-permute-start | bytes 98312 | tf_op jit(solution)/shard_map/ppermute | solution.py:208
  26.6 10.1 %all_to_all.16.refs_0_ = f32[32,1,128]{2,1,0:T(1,128)S(1)} all-to-all(f32[32,1,128]{2,1,0:T(1,128)} %get-tuple-element.15), channel_id=1, replica_groups=mesh['dp'=8,'outer'=4] {'dp','outer'}, dimensions={0} | all-to-all | bytes 32768 | tf_op jit(solution)/shard_map/all_to_all | solution.py:240
  36.7 0.0 collective-permute-done.2.refs_8_
  36.7 0.0 collective-permute-done.1.refs_7_
  36.7 0.0 collective-permute-done.refs_6_
  36.8 0.2 shard_map.111
  37.0 9.6 %all_to_all.17 = bf16[8,128,128]{2,1,0:T(8,128)(2,1)S(1)} all-to-all(bf16[8,128,128]{2,1,0:T(8,128)(2,1)S(1)} %shard_map.111), channel_id=1, replica_groups={{8,28,24,4,0,20,12,16},{9,29,25,5,1,21,13,17},{10,30,26,6,2,22,14,18},{..., dimensions={0} | all-to-all | bytes 524288 | tf_op jit(solution)/shard_map/all_to_all | solution.py:252
  46.7 0.1 reshape.67.mine_ref
  46.8 0.1 collective-permute-start.3
  46.9 1.0 %shard_map.110 = (f32[2,128,128]{2,1,0:T(8,128)}, bf16[2,128,128]{2,1,0:T(8,128)(2,1)}, bf16[2,128,128]{2,1,0:T(8,128)(2,1)}, f32[2,2,4]{2,1,0:T(2,128)}, f32[2,2,4]{2,1,0:T(2,128)}) custom-call(f32[32,1,128]{2,1,0:T(1,128)S(1)} %all_to_all.16.refs_0_, f32[2,128,128]{2,1,0:T(8,128)S(1)} %bitcast.41, bf16[2,128,128]{2,1,0:T(8,128)(2,1)S(1)} %bitcast.43, ...), custom_call_target="tpu_custom_call" | custom-call | tf_op jit(solution)/shard_map/pallas_call | solution.py:181
  47.9 0.5 %collective-permute-done.3.other_ref = bf16[16,8192]{1,0:T(8,128)(2,1)S(1)} collective-permute-done((bf16[16,8192]{1,0:T(8,128)(2,1)S(1)}, bf16[16,8192]{1,0:T(8,128)(2,1)S(1)}, u32[]{:S(2)}, u32[]{:S(2)}) %collective-permute-start.3) | collective-permute-done | bytes 262176 | tf_op jit(solution)/shard_map/ppermute | solution.py:208
  48.4 0.8 %shard_map.112 = bf16[2,16,8192]{2,1,0:T(8,128)(2,1)} custom-call(bf16[16,8192]{1,0:T(8,128)(2,1)S(1)} %reshape.67.mine_ref, bf16[16,8192]{1,0:T(8,128)(2,1)S(1)} %collective-permute-done.3.other_ref), custom_call_target="tpu_custom_call" | custom-call | tf_op jit(solution)/shard_map/pallas_call | solution.py:181
  (18 shorter events, 0.2 us)
Async XLA Ops:
  2.1 21.9 %copy-start.2 = (bf16[2,2,8192]{2,1,0:T(2,128)(2,1)S(1)}, bf16[2,2,8192]{2,1,0:T(2,128)(2,1)}, u32[]{:S(2)}) copy-start(bf16[2,2,8192]{2,1,0:T(2,128)(2,1)} %param.9) | copy-start | bytes 196612
  2.1 21.9 %copy-start.3 = (f32[2,2,4]{2,1,0:T(2,128)S(1)}, f32[2,2,4]{2,1,0:T(2,128)}, u32[]{:S(2)}) copy-start(f32[2,2,4]{2,1,0:T(2,128)} %ms_ref.1) | copy-start | bytes 196
  2.1 21.9 %copy-start.4 = (f32[2,2,4]{2,1,0:T(2,128)S(1)}, f32[2,2,4]{2,1,0:T(2,128)}, u32[]{:S(2)}) copy-start(f32[2,2,4]{2,1,0:T(2,128)} %vs_ref.1) | copy-start | bytes 196
  24.0 12.8 %copy-start = (f32[2,2,8192]{2,1,0:T(2,128)S(1)}, f32[2,2,8192]{2,1,0:T(2,128)}, u32[]{:S(2)}) copy-start(f32[2,2,8192]{2,1,0:T(2,128)} %param.7) | copy-start | bytes 393220
  24.0 12.8 %copy-start.1 = (bf16[2,2,8192]{2,1,0:T(2,128)(2,1)S(1)}, bf16[2,2,8192]{2,1,0:T(2,128)(2,1)}, u32[]{:S(2)}) copy-start(bf16[2,2,8192]{2,1,0:T(2,128)(2,1)} %param.8) | copy-start | bytes 196612
  24.7 12.0 %collective-permute-start.2 = (f32[64,128]{1,0:T(8,128)S(1)}, f32[64,128]{1,0:T(8,128)S(1)}, u32[]{:S(2)}, u32[]{:S(2)}) collective-permute-start(f32[64,128]{1,0:T(8,128)S(1)} %get-tuple-element.18.refs_5_), channel_id=1, source_target_pairs={{0,3},{1,2},{2,1},{3,0},{4,7},{5,6},{6,5},{7,4},{8,11},{9,10},{10,... | collective-permute-start | bytes 98312 | tf_op jit(solution)/shard_map/ppermute | solution.py:208
  25.2 11.5 %collective-permute-start.1 = (f32[64,128]{1,0:T(8,128)S(1)}, f32[64,128]{1,0:T(8,128)S(1)}, u32[]{:S(2)}, u32[]{:S(2)}) collective-permute-start(f32[64,128]{1,0:T(8,128)S(1)} %get-tuple-element.18.refs_5_), channel_id=1, source_target_pairs={{0,2},{1,3},{2,0},{3,1},{4,6},{5,7},{6,4},{7,5},{8,10},{9,11},{10,... | collective-permute-start | bytes 98312 | tf_op jit(solution)/shard_map/ppermute | solution.py:208
  26.0 10.8 %collective-permute-start = (f32[64,128]{1,0:T(8,128)S(1)}, f32[64,128]{1,0:T(8,128)S(1)}, u32[]{:S(2)}, u32[]{:S(2)}) collective-permute-start(f32[64,128]{1,0:T(8,128)S(1)} %get-tuple-element.18.refs_5_), channel_id=1, source_target_pairs={{0,1},{1,0},{2,3},{3,2},{4,5},{5,4},{6,7},{7,6},{8,9},{9,8},{10,11... | collective-permute-start | bytes 98312 | tf_op jit(solution)/shard_map/ppermute | solution.py:208
  46.8 1.6 %collective-permute-start.3 = (bf16[16,8192]{1,0:T(8,128)(2,1)S(1)}, bf16[16,8192]{1,0:T(8,128)(2,1)S(1)}, u32[]{:S(2)}, u32[]{:S(2)}) collective-permute-start(bf16[16,8192]{1,0:T(8,128)(2,1)S(1)} %reshape.67.mine_ref), channel_id=1, source_target_pairs={{0,1},{1,0},{2,3},{3,2},{4,5},{5,4},{6,7},{7,6},{8,9},{9,8},{10,11... | collective-permute-start | bytes 786440 | tf_op jit(solution)/shard_map/ppermute | solution.py:208

commit v5 on v4

--- a/solution.py
+++ b/solution.py
@@ -34,6 +34,16 @@
 
 def inverse(parts):
     return tuple(parts.index(i) for i in range(len(parts)))
+
+
+def cut_kernel(places, rows, own_ref, pieces_ref):
+    count = own_ref.shape[0]
+    part = pieces_ref.shape[1] // (count * rows)
+    for place, (d, o) in enumerate(places):
+        for at in range(count):
+            for row in range(rows):
+                there = pl.ds((at * rows + row) * part, part)
+                pieces_ref[place, there, :] = own_ref[at, d * rows + row, pl.ds(o * part, part), :]
 
 
 def sum_kernel(got_ref, v_ref, ms_ref, vs_ref, piece_ref, square_ref, scale_ref, v_out_ref):
@@ -221,12 +231,14 @@
         tall = (count, tiles * rows, LANES)
         vmem, far = pl.BlockSpec(memory_space=pltpu.VMEM), pl.BlockSpec(memory_space=pl.ANY)
         shape_of = jax.ShapeDtypeStruct
-        pieces = own.reshape(count, dp_n, rows, outer_n, part, LANES)
-        pieces = arrange(pieces.transpose(1, 3, 0, 2, 4, 5), SHARE_EIGHTHS)
-        pieces = arrange(pieces.transpose(1, 0, 2, 3, 4, 5), SHARE_QUARTERS)
-        pieces = pieces.reshape(total_n, count * rows * part, LANES)
         share_dp, share_outer = ordered(dp_n, SHARE_EIGHTHS), ordered(outer_n, SHARE_QUARTERS)
-        share = [d * outer_n + o for o in share_outer for d in share_dp]
+        places = [(d, o) for o in share_outer for d in share_dp]
+        share = [d * outer_n + o for d, o in places]
+        (pieces,) = call(
+            lambda *refs: cut_kernel(places, rows, *refs),
+            [near_shape((total_n, count * rows * part, LANES), bf16)],
+            [near(own.reshape(count, rows_all, tiles, LANES))],
+        )
         got = lax.all_to_all(pieces, BOTH, 0, 0, axis_index_groups=[share], tiled=True)
         blocks = m_scales.shape[2]
         piece, square, scales, v_part = call(

time: 49.5 us -> 49.3 us (level)
    unnamed x21 -> x17, local copies, waits for them, and re-layouts: 1.32 us -> 1.25 us
    pallas_call x4 -> x5, Pallas kernels: 2.72 us -> 2.75 us  [call(): pl.pallas_call(kernel, out_shape=outs, in_specs=in_specs or [spec] * len(...]
where the time goes in v5:
time: 49.3 us; the launch traced here: 49 us
  blocking collectives  41.6 us (84%)
  Pallas kernels  2.75 us (6%)
  starting transfers between devices  1.93 us (4%)
  local copies, waits for them, and re-layouts  1.37 us (3%)
  between operations  0.76 us (2%)
  waiting for transfers between devices  0.54 us (1%)
    all_to_all x1, blocking collectives, body(): lax.all_to_all(pieces, BOTH, 0, 0, axis_index_groups=[share], tiled=True)  21.8 us
    all_to_all x1, blocking collectives, body(): squares = lax.all_to_all(square, BOTH, 0, 0, tiled=True)  10.1 us
    all_to_all x1, blocking collectives, body(): lax.all_to_all(mine, 'dp', 0, 0, axis_index_groups=[spread], tiled=True)  9.65 us
    pallas_call x5, Pallas kernels, call(): pl.pallas_call(kernel, out_shape=outs, in_specs=in_specs or [spec] * len(...  2.75 us
    ppermute x4, starting transfers between devices, flip(): return lax.ppermute(value, 'outer', [(i, i ^ bit) for i in range(size)])  1.93 us
    unnamed x17, local copies, waits for them, and re-layouts  1.25 us
  transfers between devices with their start and end apart: 4, of which 1 were waited for; matrix products, arithmetic and copies ran while one was open for 0% of the time, Pallas kernels for 2%

profile of v5, /device:TPU:0, one launch (start us, length us, event | category | flops | bytes accessed | tf_op | source)
XLA Modules:
  0.0 49.0 jit_solution(2927660677508801476)
XLA Ops:
  0.6 1.2 %copy.18 = bf16[4,8,64,128]{3,2,1,0:T(8,128)(2,1)S(1)} copy(bf16[4,8,64,128]{3,1,2,0:T(8,128)(2,1)} %bitcast.41) | data formatting | bytes 1048576
  1.8 0.0 copy-start.2
  1.9 0.0 copy-start.3
  1.9 0.0 copy-start.4
  1.9 21.8 %all_to_all.15.got_ref = bf16[32,64,128]{2,1,0:T(8,128)(2,1)S(1)} all-to-all(bf16[32,64,128]{2,1,0:T(8,128)(2,1)S(1)} %shard_map.109), channel_id=1, replica_groups={{11,15,3,19,23,27,7,31,9,13,1,17,21,25,5,29,8,12,0,16,20,24,4,28,10,14,..., dimensions={0} | all-to-all | bytes 1048576 | tf_op jit(solution)/shard_map/all_to_all | solution.py:242
  23.7 0.0 copy-start
  23.7 0.0 copy-start.1
  23.7 0.7 %shard_map.110 = (f32[64,128]{1,0:T(8,128)S(1)}, f32[32,1,128]{2,1,0:T(1,128)}, f32[2,4,8,128]{3,2,1,0:T(8,128)S(1)}, f32[2,128,128]{2,1,0:T(8,128)S(1)}) custom-call(bf16[32,64,128]{2,1,0:T(8,128)(2,1)S(1)} %all_to_all.15.got_ref, bf16[2,128,128]{2,1,0:T(8,128)(2,1)S(1)} %bitcast.40, f32[2,2,4]{2,1,0:T(2,128)S(1)} %copy-done.3, f32[2,2,4]{2,1,0:T(2,128)S(1)} %copy-done.4), custom_call_target="tpu_custom_call" | custom-call | tf_op jit(solution)/shard_map/pallas_call | solution.py:191
  24.5 0.5 %collective-permute-start.2 = (f32[64,128]{1,0:T(8,128)S(1)}, f32[64,128]{1,0:T(8,128)S(1)}, u32[]{:S(2)}, u32[]{:S(2)}) collective-permute-start(f32[64,128]{1,0:T(8,128)S(1)} %get-tuple-element.18.refs_5_), channel_id=1, source_target_pairs={{0,3},{1,2},{2,1},{3,0},{4,7},{5,6},{6,5},{7,4},{8,11},{9,10},{10,... | collective-permute-start | bytes 98312 | tf_op jit(solution)/shard_map/ppermute | solution.py:218
  25.0 0.7 %collective-permute-start.1 = (f32[64,128]{1,0:T(8,128)S(1)}, f32[64,128]{1,0:T(8,128)S(1)}, u32[]{:S(2)}, u32[]{:S(2)}) collective-permute-start(f32[64,128]{1,0:T(8,128)S(1)} %get-tuple-element.18.refs_5_), channel_id=1, source_target_pairs={{0,2},{1,3},{2,0},{3,1},{4,6},{5,7},{6,4},{7,5},{8,10},{9,11},{10,... | collective-permute-start | bytes 98312 | tf_op jit(solution)/shard_map/ppermute | solution.py:218
  25.7 0.6 %collective-permute-start = (f32[64,128]{1,0:T(8,128)S(1)}, f32[64,128]{1,0:T(8,128)S(1)}, u32[]{:S(2)}, u32[]{:S(2)}) collective-permute-start(f32[64,128]{1,0:T(8,128)S(1)} %get-tuple-element.18.refs_5_), channel_id=1, source_target_pairs={{0,1},{1,0},{2,3},{3,2},{4,5},{5,4},{6,7},{7,6},{8,9},{9,8},{10,11... | collective-permute-start | bytes 98312 | tf_op jit(solution)/shard_map/ppermute | solution.py:218
  26.3 10.1 %all_to_all.16.refs_0_ = f32[32,1,128]{2,1,0:T(1,128)S(1)} all-to-all(f32[32,1,128]{2,1,0:T(1,128)} %get-tuple-element.15), channel_id=1, replica_groups=mesh['dp'=8,'outer'=4] {'dp','outer'}, dimensions={0} | all-to-all | bytes 32768 | tf_op jit(solution)/shard_map/all_to_all | solution.py:252
  36.5 0.0 collective-permute-done.2.refs_8_
  36.5 0.0 collective-permute-done.1.refs_7_
  36.5 0.0 collective-permute-done.refs_6_
  36.5 0.0 copy-done
  36.5 0.0 copy-done.1
  36.5 0.2 shard_map.112
  36.7 9.6 %all_to_all.17 = bf16[8,128,128]{2,1,0:T(8,128)(2,1)S(1)} all-to-all(bf16[8,128,128]{2,1,0:T(8,128)(2,1)S(1)} %shard_map.112), channel_id=1, replica_groups={{8,28,24,4,0,20,12,16},{9,29,25,5,1,21,13,17},{10,30,26,6,2,22,14,18},{..., dimensions={0} | all-to-all | bytes 524288 | tf_op jit(solution)/shard_map/all_to_all | solution.py:264
  46.4 0.1 reshape.63.mine_ref
  46.6 0.1 collective-permute-start.3
  46.7 1.0 %shard_map.111 = (f32[2,128,128]{2,1,0:T(8,128)}, bf16[2,128,128]{2,1,0:T(8,128)(2,1)}, bf16[2,128,128]{2,1,0:T(8,128)(2,1)}, f32[2,2,4]{2,1,0:T(2,128)}, f32[2,2,4]{2,1,0:T(2,128)}) custom-call(f32[32,1,128]{2,1,0:T(1,128)S(1)} %all_to_all.16.refs_0_, f32[2,128,128]{2,1,0:T(8,128)S(1)} %bitcast.37, bf16[2,128,128]{2,1,0:T(8,128)(2,1)S(1)} %bitcast.39, ...), custom_call_target="tpu_custom_call" | custom-call | tf_op jit(solution)/shard_map/pallas_call | solution.py:191
  47.6 0.5 %collective-permute-done.3.other_ref = bf16[16,8192]{1,0:T(8,128)(2,1)S(1)} collective-permute-done((bf16[16,8192]{1,0:T(8,128)(2,1)S(1)}, bf16[16,8192]{1,0:T(8,128)(2,1)S(1)}, u32[]{:S(2)}, u32[]{:S(2)}) %collective-permute-start.3) | collective-permute-done | bytes 262176 | tf_op jit(solution)/shard_map/ppermute | solution.py:218
  48.2 0.8 %shard_map.113 = bf16[2,16,8192]{2,1,0:T(8,128)(2,1)} custom-call(bf16[16,8192]{1,0:T(8,128)(2,1)S(1)} %reshape.63.mine_ref, bf16[16,8192]{1,0:T(8,128)(2,1)S(1)} %collective-permute-done.3.other_ref), custom_call_target="tpu_custom_call" | custom-call | tf_op jit(solution)/shard_map/pallas_call | solution.py:191
  (11 shorter events, 0.1 us)
Async XLA Ops:
  1.8 21.9 %copy-start.2 = (bf16[2,2,8192]{2,1,0:T(2,128)(2,1)S(1)}, bf16[2,2,8192]{2,1,0:T(2,128)(2,1)}, u32[]{:S(2)}) copy-start(bf16[2,2,8192]{2,1,0:T(2,128)(2,1)} %param.9) | copy-start | bytes 196612
  1.9 21.9 %copy-start.3 = (f32[2,2,4]{2,1,0:T(2,128)S(1)}, f32[2,2,4]{2,1,0:T(2,128)}, u32[]{:S(2)}) copy-start(f32[2,2,4]{2,1,0:T(2,128)} %ms_ref.1) | copy-start | bytes 196
  1.9 21.9 %copy-start.4 = (f32[2,2,4]{2,1,0:T(2,128)S(1)}, f32[2,2,4]{2,1,0:T(2,128)}, u32[]{:S(2)}) copy-start(f32[2,2,4]{2,1,0:T(2,128)} %vs_ref.1) | copy-start | bytes 196
  23.7 12.8 %copy-start = (f32[2,2,8192]{2,1,0:T(2,128)S(1)}, f32[2,2,8192]{2,1,0:T(2,128)}, u32[]{:S(2)}) copy-start(f32[2,2,8192]{2,1,0:T(2,128)} %param.7) | copy-start | bytes 393220
  23.7 12.8 %copy-start.1 = (bf16[2,2,8192]{2,1,0:T(2,128)(2,1)S(1)}, bf16[2,2,8192]{2,1,0:T(2,128)(2,1)}, u32[]{:S(2)}) copy-start(bf16[2,2,8192]{2,1,0:T(2,128)(2,1)} %param.8) | copy-start | bytes 196612
  24.5 12.0 %collective-permute-start.2 = (f32[64,128]{1,0:T(8,128)S(1)}, f32[64,128]{1,0:T(8,128)S(1)}, u32[]{:S(2)}, u32[]{:S(2)}) collective-permute-start(f32[64,128]{1,0:T(8,128)S(1)} %get-tuple-element.18.refs_5_), channel_id=1, source_target_pairs={{0,3},{1,2},{2,1},{3,0},{4,7},{5,6},{6,5},{7,4},{8,11},{9,10},{10,... | collective-permute-start | bytes 98312 | tf_op jit(solution)/shard_map/ppermute | solution.py:218
  25.0 11.5 %collective-permute-start.1 = (f32[64,128]{1,0:T(8,128)S(1)}, f32[64,128]{1,0:T(8,128)S(1)}, u32[]{:S(2)}, u32[]{:S(2)}) collective-permute-start(f32[64,128]{1,0:T(8,128)S(1)} %get-tuple-element.18.refs_5_), channel_id=1, source_target_pairs={{0,2},{1,3},{2,0},{3,1},{4,6},{5,7},{6,4},{7,5},{8,10},{9,11},{10,... | collective-permute-start | bytes 98312 | tf_op jit(solution)/shard_map/ppermute | solution.py:218
  25.7 10.8 %collective-permute-start = (f32[64,128]{1,0:T(8,128)S(1)}, f32[64,128]{1,0:T(8,128)S(1)}, u32[]{:S(2)}, u32[]{:S(2)}) collective-permute-start(f32[64,128]{1,0:T(8,128)S(1)} %get-tuple-element.18.refs_5_), channel_id=1, source_target_pairs={{0,1},{1,0},{2,3},{3,2},{4,5},{5,4},{6,7},{7,6},{8,9},{9,8},{10,11... | collective-permute-start | bytes 98312 | tf_op jit(solution)/shard_map/ppermute | solution.py:218
  46.6 1.6 %collective-permute-start.3 = (bf16[16,8192]{1,0:T(8,128)(2,1)S(1)}, bf16[16,8192]{1,0:T(8,128)(2,1)S(1)}, u32[]{:S(2)}, u32[]{:S(2)}) collective-permute-start(bf16[16,8192]{1,0:T(8,128)(2,1)S(1)} %reshape.63.mine_ref), channel_id=1, source_target_pairs={{0,1},{1,0},{2,3},{3,2},{4,5},{5,4},{6,7},{7,6},{8,9},{9,8},{10,11... | collective-permute-start | bytes 786440 | tf_op jit(solution)/shard_map/ppermute | solution.py:218

commit v6 on v5

--- a/solution.py
+++ b/solution.py
@@ -25,17 +25,6 @@
     return [part * span + i for part in parts for i in range(span)]
 
 
-def arrange(value, parts):
-    if value.shape[0] % len(parts):
-        return value
-    blocks = jnp.split(value, len(parts), axis=0)
-    return jnp.concatenate([blocks[part] for part in parts], axis=0)
-
-
-def inverse(parts):
-    return tuple(parts.index(i) for i in range(len(parts)))
-
-
 def cut_kernel(places, rows, own_ref, pieces_ref):
     count = own_ref.shape[0]
     part = pieces_ref.shape[1] // (count * rows)
@@ -44,6 +33,11 @@
             for row in range(rows):
                 there = pl.ds((at * rows + row) * part, part)
                 pieces_ref[place, there, :] = own_ref[at, d * rows + row, pl.ds(o * part, part), :]
+
+
+def line_up_kernel(order, got_ref, lined_ref):
+    for place, member in enumerate(order):
+        lined_ref[member] = got_ref[place]
 
 
 def sum_kernel(got_ref, v_ref, ms_ref, vs_ref, piece_ref, square_ref, scale_ref, v_out_ref):
@@ -262,7 +256,11 @@
         )
         spread = ordered(dp_n, SPREAD_EIGHTHS)
         mine = lax.all_to_all(mine, "dp", 0, 0, axis_index_groups=[spread], tiled=True)
-        mine = arrange(mine, inverse(SPREAD_EIGHTHS)).reshape(rows_all, width)
+        (mine,) = call(
+            lambda *refs: line_up_kernel(spread, *refs),
+            [near_shape(mine.shape, bf16)], [near(mine)],
+        )
+        mine = mine.reshape(rows_all, width)
         half_spec = vmem if is_small(mine) else far
         other = flip(mine, outer_n, 1)
         fresh, m_next, v_next, m_top, v_top = call(

time: 49.3 us -> 49.2 us (level)
    unnamed x17 -> x11, local copies, waits for them, and re-layouts: 1.25 us -> 1.19 us
    pallas_call x5 -> x6, Pallas kernels: 2.75 us -> 2.77 us  [call(): pl.pallas_call(kernel, out_shape=outs, in_specs=in_specs or [spec] * len(...]
where the time goes in v6:
time: 49.2 us; the launch traced here: 48.9 us
  blocking collectives  41.6 us (85%)
  Pallas kernels  2.77 us (6%)
  starting transfers between devices  1.93 us (4%)
  local copies, waits for them, and re-layouts  1.3 us (3%)
  between operations  0.74 us (2%)
  waiting for transfers between devices  0.54 us (1%)
    all_to_all x1, blocking collectives, body(): lax.all_to_all(pieces, BOTH, 0, 0, axis_index_groups=[share], tiled=True)  21.8 us
    all_to_all x1, blocking collectives, body(): squares = lax.all_to_all(square, BOTH, 0, 0, tiled=True)  10.1 us
    all_to_all x1, blocking collectives, body(): lax.all_to_all(mine, 'dp', 0, 0, axis_index_groups=[spread], tiled=True)  9.65 us
    pallas_call x6, Pallas kernels, call(): pl.pallas_call(kernel, out_shape=outs, in_specs=in_specs or [spec] * len(...  2.77 us
    ppermute x4, starting transfers between devices, flip(): return lax.ppermute(value, 'outer', [(i, i ^ bit) for i in range(size)])  1.93 us
    unnamed x11, local copies, waits for them, and re-layouts  1.19 us
  transfers between devices with their start and end apart: 4, of which 1 were waited for; matrix products, arithmetic and copies ran while one was open for 0% of the time, Pallas kernels for 2%

profile of v6, /device:TPU:0, one launch (start us, length us, event | category | flops | bytes accessed | tf_op | source)
XLA Modules:
  0.0 48.9 jit_solution(8531648829051655468)
XLA Ops:
  0.6 1.2 %copy.18 = bf16[4,8,64,128]{3,2,1,0:T(8,128)(2,1)S(1)} copy(bf16[4,8,64,128]{3,1,2,0:T(8,128)(2,1)} %bitcast.41) | data formatting | bytes 1048576
  1.8 0.0 copy-start.2
  1.9 0.0 copy-start.3
  1.9 0.0 copy-start.4
  1.9 21.8 %all_to_all.15.got_ref = bf16[32,64,128]{2,1,0:T(8,128)(2,1)S(1)} all-to-all(bf16[32,64,128]{2,1,0:T(8,128)(2,1)S(1)} %shard_map.109), channel_id=1, replica_groups={{11,15,3,19,23,27,7,31,9,13,1,17,21,25,5,29,8,12,0,16,20,24,4,28,10,14,..., dimensions={0} | all-to-all | bytes 1048576 | tf_op jit(solution)/shard_map/all_to_all | solution.py:236
  23.7 0.0 copy-start
  23.7 0.0 copy-start.1
  23.7 0.7 %shard_map.110 = (f32[64,128]{1,0:T(8,128)S(1)}, f32[32,1,128]{2,1,0:T(1,128)}, f32[2,4,8,128]{3,2,1,0:T(8,128)S(1)}, f32[2,128,128]{2,1,0:T(8,128)S(1)}) custom-call(bf16[32,64,128]{2,1,0:T(8,128)(2,1)S(1)} %all_to_all.15.got_ref, bf16[2,128,128]{2,1,0:T(8,128)(2,1)S(1)} %bitcast.40, f32[2,2,4]{2,1,0:T(2,128)S(1)} %copy-done.3, f32[2,2,4]{2,1,0:T(2,128)S(1)} %copy-done.4), custom_call_target="tpu_custom_call" | custom-call | tf_op jit(solution)/shard_map/pallas_call | solution.py:185
  24.5 0.5 %collective-permute-start.2 = (f32[64,128]{1,0:T(8,128)S(1)}, f32[64,128]{1,0:T(8,128)S(1)}, u32[]{:S(2)}, u32[]{:S(2)}) collective-permute-start(f32[64,128]{1,0:T(8,128)S(1)} %get-tuple-element.18.refs_5_), channel_id=1, source_target_pairs={{0,3},{1,2},{2,1},{3,0},{4,7},{5,6},{6,5},{7,4},{8,11},{9,10},{10,... | collective-permute-start | bytes 98312 | tf_op jit(solution)/shard_map/ppermute | solution.py:212
  25.0 0.7 %collective-permute-start.1 = (f32[64,128]{1,0:T(8,128)S(1)}, f32[64,128]{1,0:T(8,128)S(1)}, u32[]{:S(2)}, u32[]{:S(2)}) collective-permute-start(f32[64,128]{1,0:T(8,128)S(1)} %get-tuple-element.18.refs_5_), channel_id=1, source_target_pairs={{0,2},{1,3},{2,0},{3,1},{4,6},{5,7},{6,4},{7,5},{8,10},{9,11},{10,... | collective-permute-start | bytes 98312 | tf_op jit(solution)/shard_map/ppermute | solution.py:212
  25.7 0.6 %collective-permute-start = (f32[64,128]{1,0:T(8,128)S(1)}, f32[64,128]{1,0:T(8,128)S(1)}, u32[]{:S(2)}, u32[]{:S(2)}) collective-permute-start(f32[64,128]{1,0:T(8,128)S(1)} %get-tuple-element.18.refs_5_), channel_id=1, source_target_pairs={{0,1},{1,0},{2,3},{3,2},{4,5},{5,4},{6,7},{7,6},{8,9},{9,8},{10,11... | collective-permute-start | bytes 98312 | tf_op jit(solution)/shard_map/ppermute | solution.py:212
  26.3 10.1 %all_to_all.16.refs_0_ = f32[32,1,128]{2,1,0:T(1,128)S(1)} all-to-all(f32[32,1,128]{2,1,0:T(1,128)} %get-tuple-element.15), channel_id=1, replica_groups=mesh['dp'=8,'outer'=4] {'dp','outer'}, dimensions={0} | all-to-all | bytes 32768 | tf_op jit(solution)/shard_map/all_to_all | solution.py:246
  36.5 0.0 collective-permute-done.2.refs_8_
  36.5 0.0 collective-permute-done.1.refs_7_
  36.5 0.0 collective-permute-done.refs_6_
  36.5 0.0 copy-done
  36.5 0.0 copy-done.1
  36.5 0.2 shard_map.112
  36.7 9.6 %all_to_all.17.refs_0_ = bf16[8,128,128]{2,1,0:T(8,128)(2,1)S(1)} all-to-all(bf16[8,128,128]{2,1,0:T(8,128)(2,1)S(1)} %shard_map.112), channel_id=1, replica_groups={{8,28,24,4,0,20,12,16},{9,29,25,5,1,21,13,17},{10,30,26,6,2,22,14,18},{..., dimensions={0} | all-to-all | bytes 524288 | tf_op jit(solution)/shard_map/all_to_all | solution.py:258
  46.4 0.1 reshape.63.mine_ref
  46.5 0.1 collective-permute-start.3
  46.6 1.0 %shard_map.111 = (f32[2,128,128]{2,1,0:T(8,128)}, bf16[2,128,128]{2,1,0:T(8,128)(2,1)}, bf16[2,128,128]{2,1,0:T(8,128)(2,1)}, f32[2,2,4]{2,1,0:T(2,128)}, f32[2,2,4]{2,1,0:T(2,128)}) custom-call(f32[32,1,128]{2,1,0:T(1,128)S(1)} %all_to_all.16.refs_0_, f32[2,128,128]{2,1,0:T(8,128)S(1)} %bitcast.37, bf16[2,128,128]{2,1,0:T(8,128)(2,1)S(1)} %bitcast.39, ...), custom_call_target="tpu_custom_call" | custom-call | tf_op jit(solution)/shard_map/pallas_call | solution.py:185
  47.6 0.5 %collective-permute-done.3.other_ref = bf16[16,8192]{1,0:T(8,128)(2,1)S(1)} collective-permute-done((bf16[16,8192]{1,0:T(8,128)(2,1)S(1)}, bf16[16,8192]{1,0:T(8,128)(2,1)S(1)}, u32[]{:S(2)}, u32[]{:S(2)}) %collective-permute-start.3) | collective-permute-done | bytes 262176 | tf_op jit(solution)/shard_map/ppermute | solution.py:212
  48.1 0.8 %shard_map.114 = bf16[2,16,8192]{2,1,0:T(8,128)(2,1)} custom-call(bf16[16,8192]{1,0:T(8,128)(2,1)S(1)} %reshape.63.mine_ref, bf16[16,8192]{1,0:T(8,128)(2,1)S(1)} %collective-permute-done.3.other_ref), custom_call_target="tpu_custom_call" | custom-call | tf_op jit(solution)/shard_map/pallas_call | solution.py:185
  (5 shorter events, 0.1 us)
Async XLA Ops:
  1.8 21.9 %copy-start.2 = (bf16[2,2,8192]{2,1,0:T(2,128)(2,1)S(1)}, bf16[2,2,8192]{2,1,0:T(2,128)(2,1)}, u32[]{:S(2)}) copy-start(bf16[2,2,8192]{2,1,0:T(2,128)(2,1)} %param.9) | copy-start | bytes 196612
  1.9 21.9 %copy-start.3 = (f32[2,2,4]{2,1,0:T(2,128)S(1)}, f32[2,2,4]{2,1,0:T(2,128)}, u32[]{:S(2)}) copy-start(f32[2,2,4]{2,1,0:T(2,128)} %ms_ref.1) | copy-start | bytes 196
  1.9 21.9 %copy-start.4 = (f32[2,2,4]{2,1,0:T(2,128)S(1)}, f32[2,2,4]{2,1,0:T(2,128)}, u32[]{:S(2)}) copy-start(f32[2,2,4]{2,1,0:T(2,128)} %vs_ref.1) | copy-start | bytes 196
  23.7 12.8 %copy-start = (f32[2,2,8192]{2,1,0:T(2,128)S(1)}, f32[2,2,8192]{2,1,0:T(2,128)}, u32[]{:S(2)}) copy-start(f32[2,2,8192]{2,1,0:T(2,128)} %param.7) | copy-start | bytes 393220
  23.7 12.8 %copy-start.1 = (bf16[2,2,8192]{2,1,0:T(2,128)(2,1)S(1)}, bf16[2,2,8192]{2,1,0:T(2,128)(2,1)}, u32[]{:S(2)}) copy-start(bf16[2,2,8192]{2,1,0:T(2,128)(2,1)} %param.8) | copy-start | bytes 196612
  24.5 12.0 %collective-permute-start.2 = (f32[64,128]{1,0:T(8,128)S(1)}, f32[64,128]{1,0:T(8,128)S(1)}, u32[]{:S(2)}, u32[]{:S(2)}) collective-permute-start(f32[64,128]{1,0:T(8,128)S(1)} %get-tuple-element.18.refs_5_), channel_id=1, source_target_pairs={{0,3},{1,2},{2,1},{3,0},{4,7},{5,6},{6,5},{7,4},{8,11},{9,10},{10,... | collective-permute-start | bytes 98312 | tf_op jit(solution)/shard_map/ppermute | solution.py:212
  25.0 11.5 %collective-permute-start.1 = (f32[64,128]{1,0:T(8,128)S(1)}, f32[64,128]{1,0:T(8,128)S(1)}, u32[]{:S(2)}, u32[]{:S(2)}) collective-permute-start(f32[64,128]{1,0:T(8,128)S(1)} %get-tuple-element.18.refs_5_), channel_id=1, source_target_pairs={{0,2},{1,3},{2,0},{3,1},{4,6},{5,7},{6,4},{7,5},{8,10},{9,11},{10,... | collective-permute-start | bytes 98312 | tf_op jit(solution)/shard_map/ppermute | solution.py:212
  25.7 10.8 %collective-permute-start = (f32[64,128]{1,0:T(8,128)S(1)}, f32[64,128]{1,0:T(8,128)S(1)}, u32[]{:S(2)}, u32[]{:S(2)}) collective-permute-start(f32[64,128]{1,0:T(8,128)S(1)} %get-tuple-element.18.refs_5_), channel_id=1, source_target_pairs={{0,1},{1,0},{2,3},{3,2},{4,5},{5,4},{6,7},{7,6},{8,9},{9,8},{10,11... | collective-permute-start | bytes 98312 | tf_op jit(solution)/shard_map/ppermute | solution.py:212
  46.5 1.6 %collective-permute-start.3 = (bf16[16,8192]{1,0:T(8,128)(2,1)S(1)}, bf16[16,8192]{1,0:T(8,128)(2,1)S(1)}, u32[]{:S(2)}, u32[]{:S(2)}) collective-permute-start(bf16[16,8192]{1,0:T(8,128)(2,1)S(1)} %reshape.63.mine_ref), channel_id=1, source_target_pairs={{0,1},{1,0},{2,3},{3,2},{4,5},{5,4},{6,7},{7,6},{8,9},{9,8},{10,11... | collective-permute-start | bytes 786440 | tf_op jit(solution)/shard_map/ppermute | solution.py:212
